TPU v7x, 256 devices: a whole 4x4x8 slice. The times are simulated.
256 devices in a mesh: lat: 64 (over z, y, x_hi), lon: 4 (over x_lo, core).
Axes of the slice: x: 4 (x_hi: 2, x_lo: 2; x = x_hi * 2 + x_lo), y: 4, z: 8, core: 2. Of those that a mesh axis runs over, the one named last changes fastest.
Arguments:
- grid_latent: bfloat16 [131072, 512], P(('lat', 'lon')), may hold values from -6 to 6
- grid_feat: bfloat16 [4, 524288], P(None, ('lat', 'lon')), may hold values from -6 to 6
- grid_sender: int32 [524288], P(('lat', 'lon')), may hold values from 0 to 511
- grid_owner: int32 [524288, 1], P(('lat', 'lon')), may hold values from 0 to 63; in each aligned block of 2048 rows (0 to 2047, 2048 to 4095, ...) at most 64 rows name the same one
- grid_node: int32 [524288], P(('lat', 'lon')), may hold values from 0 to 511
- mesh_latent: bfloat16 [32768, 512], P('lat', 'lon'), may hold values from -6 to 6
- mesh_edge: bfloat16 [262144, 512], P(('lat', 'lon')), may hold values from -6 to 6
- halo_send: int32 [4096, 8], P('lat'), may hold values from 0 to 511
- mesh_sender: int32 [262144], P(('lat', 'lon')), may hold values from 0 to 1023
- mesh_receiver: int32 [262144], P(('lat', 'lon')), may hold values from 0 to 511
- enc_edge_in: bfloat16 [512, 512], P(None, 'lon'), may hold values from -0.25 to 0.25
- enc_feat_proj: bfloat16 [4, 512], replicated, may hold values from -3 to 3
- enc_edge_out: bfloat16 [512, 512], P(None, 'lon'), may hold values from -0.25 to 0.25
- enc_edge_bias: float32 [2, 512], replicated, may hold values from -1.5 to 1.5
- enc_edge_gain: float32 [512], replicated, may hold values from 0.25 to 1.75
- enc_node_in: bfloat16 [1024, 512], P(None, 'lon'), may hold values from -0.1875 to 0.1875
- enc_node_out: bfloat16 [512, 512], P('lon'), may hold values from -0.25 to 0.25
- enc_node_bias: float32 [2, 512], replicated, may hold values from -1.5 to 1.5
- enc_node_gain: float32 [512], replicated, may hold values from 0.25 to 1.75
- proc_edge_in: bfloat16 [1536, 512], P(None, 'lon'), may hold values from -0.15625 to 0.15625
- proc_edge_out: bfloat16 [512, 512], P(None, 'lon'), may hold values from -0.25 to 0.25
- proc_edge_bias: float32 [2, 512], replicated, may hold values from -1.5 to 1.5
- proc_edge_gain: float32 [512], replicated, may hold values from 0.25 to 1.75
- proc_node_in: bfloat16 [1024, 512], P(None, 'lon'), may hold values from -0.1875 to 0.1875
- proc_node_out: bfloat16 [512, 512], P('lon'), may hold values from -0.25 to 0.25
- proc_node_bias: float32 [2, 512], replicated, may hold values from -1.5 to 1.5
- proc_node_gain: float32 [512], replicated, may hold values from 0.25 to 1.75
Outputs:
- mesh_update: bfloat16 [32768, 512], P('lat', 'lon')
- edge_update: bfloat16 [262144, 512], P(('lat', 'lon'))
Inputs may be any that keep to these rules, and one draw needn't show every extreme that they name: `grid_sender`: a row among the 512 grid rows of the device that holds the edge. `grid_owner`: among the 2048 edges of one device, at most 64 name the same partition, a bound that some block reaches. `halo_send`: nodes of the listing partition.
All inputs are finite; a program needn't handle non-finite values.
Results may differ from a plain program's by a relative error of at most 0.017.
Values may be sent and summed in bfloat16 or wider, within the bound.
A program may use at most 128 MiB of HBM per device.

v0:
```python
import jax
import jax.numpy as jnp
from jax import lax
from jax.sharding import PartitionSpec as P


def side_by_side(arrays, axis, dim, along):
    both = jnp.concatenate(arrays, axis=along)
    result, at, finished = (lax.all_gather(both, axis, axis=dim, tiled=True), 0, [])
    for a in arrays:
        finished.append(lax.slice_in_dim(result, at, at + a.shape[along], axis=along))
        at += a.shape[along]
    return tuple(finished)


def sent_to_all(value, axis):
    copies = jnp.broadcast_to(value, (lax.axis_size(axis), *value.shape))
    return lax.all_to_all(copies, axis, split_axis=0, concat_axis=0, tiled=True)


def taken_together(value, axis):
    return sent_to_all(value, axis).astype(jnp.float32).sum(axis=0)


def laid_out(tiles, dim):
    dims = list(tiles.shape[1:])
    dims[dim] *= tiles.shape[0]
    return jnp.moveaxis(tiles, 0, dim).reshape(dims)


def collect(value, axis, dim):
    tiles = sent_to_all(value, axis)
    return laid_out(tiles, dim)


def layer_norm(values, norm_gain, offsets):
    average = jnp.mean(values, axis=-1, keepdims=True)
    centred = values - average
    spread = jnp.mean(centred * centred, axis=-1, keepdims=True)
    return centred * lax.rsqrt(spread + 1e-05) * norm_gain + offsets


def encoder_edges(source_rows, feat_term, weight_in, weight_out):
    piece_in, piece_out = side_by_side((weight_in, weight_out), "lon", 1, 0)
    pre_act = jnp.dot(source_rows, piece_in, preferred_element_type=jnp.float32)
    pre_act = pre_act + feat_term
    hidden = jax.nn.silu(pre_act).astype(jnp.bfloat16)
    return lax.dot_general(
        hidden, piece_out, (((1,), (1,)), ((), ())), preferred_element_type=jnp.float32
    )


def node_network(base, aggregate, weight_in, weight_out, biases, norm_gain):
    inputs = jnp.concatenate([base, aggregate], 1)
    columns = weight_in.shape[1]
    hidden_bias = lax.dynamic_slice_in_dim(biases[0], lax.axis_index("lon") * columns, columns)
    hidden = jax.nn.silu(
        jnp.dot(inputs, weight_in, preferred_element_type=jnp.float32) + hidden_bias
    ).astype(jnp.bfloat16)
    raw_out = taken_together(
        jnp.dot(hidden, weight_out, preferred_element_type=jnp.float32).astype(jnp.bfloat16), "lon"
    ).astype(jnp.float32)
    return (base.astype(jnp.float32) + layer_norm(raw_out, norm_gain, biases[1])).astype(
        jnp.bfloat16
    )


def local(
    grid_latent,
    grid_feat,
    grid_sender,
    grid_owner,
    grid_node,
    mesh_latent,
    mesh_edge,
    halo_send,
    mesh_sender,
    mesh_receiver,
    enc_edge_in,
    enc_feat_proj,
    enc_edge_out,
    enc_edge_bias,
    enc_edge_gain,
    enc_node_in,
    enc_node_out,
    enc_node_bias,
    enc_node_gain,
    proc_edge_in,
    proc_edge_out,
    proc_edge_bias,
    proc_edge_gain,
    proc_node_in,
    proc_node_out,
    proc_node_bias,
    proc_node_gain,
):
    lat_count = lax.axis_size("lat")
    lon_index = lax.axis_index("lon")
    feature_width = grid_latent.shape[1]
    quarter = mesh_latent.shape[1]
    mesh_rows = mesh_latent.shape[0]
    edge_count = grid_sender.shape[0]
    capacity = max(2, 2 * edge_count // lat_count)
    slot_total = lat_count * capacity
    owners = grid_owner[:, 0]
    owner_hits = (owners[:, None] == jnp.arange(lat_count, dtype=jnp.int32)[None, :]).astype(
        jnp.int32
    )
    slot_rank = jnp.sum((jnp.cumsum(owner_hits, axis=0) - owner_hits) * owner_hits, axis=1)
    slot_index = owners * capacity + slot_rank
    node_slots = (
        jnp.full((slot_total,), -1, jnp.int32)
        .at[slot_index]
        .set(grid_node)
        .reshape(lat_count, capacity)
    )
    source_rows = grid_latent[grid_sender]
    feat_term = (
        lax.dot_general(
            grid_feat, enc_feat_proj, (((0,), (0,)), ((), ())), preferred_element_type=jnp.float32
        )
        + enc_edge_bias[0]
    )
    raw_out = encoder_edges(source_rows, feat_term, enc_edge_in, enc_edge_out)
    messages = layer_norm(raw_out, enc_edge_gain, enc_edge_bias[1])
    buffer = (
        jnp.zeros((slot_total, feature_width), jnp.float32)
        .at[slot_index]
        .set(messages)
        .reshape(lat_count, capacity, feature_width)
    )
    arrived, node_ids = (
        lax.all_to_all(
            buffer.astype(jnp.bfloat16), "lat", split_axis=0, concat_axis=0, tiled=True
        ).astype(buffer.dtype),
        lax.all_to_all(node_slots, "lat", split_axis=0, concat_axis=0, tiled=True),
    )
    arrived = arrived.reshape(slot_total, feature_width)
    node_ids = node_ids.reshape(slot_total)
    segment_ids = jnp.where(node_ids < 0, mesh_rows, node_ids).astype(jnp.int32)
    partial_sum = jax.ops.segment_sum(arrived, segment_ids, num_segments=mesh_rows + 1)[:mesh_rows]
    gathered = taken_together(partial_sum.astype(jnp.bfloat16), "lon").astype(jnp.float32)
    mesh_full = collect(mesh_latent, "lon", 1)
    mesh_mid = node_network(
        mesh_full,
        gathered.astype(jnp.bfloat16),
        enc_node_in,
        enc_node_out,
        enc_node_bias,
        enc_node_gain,
    )
    outgoing = mesh_mid[halo_send]
    received = lax.all_to_all(outgoing, "lat", split_axis=0, concat_axis=0, tiled=True)
    table = jnp.concatenate([mesh_mid, received.reshape(-1, feature_width)], 0)
    sender_rows = table[mesh_sender]
    receiver_rows = mesh_mid[mesh_receiver]
    piece_in, piece_out = side_by_side((proc_edge_in, proc_edge_out), "lon", 1, 0)
    pre_act = jnp.dot(mesh_edge, piece_in[:feature_width], preferred_element_type=jnp.float32)
    pre_act = pre_act + jnp.dot(
        sender_rows, piece_in[feature_width : 2 * feature_width], preferred_element_type=jnp.float32
    )
    pre_act = pre_act + jnp.dot(
        receiver_rows, piece_in[2 * feature_width :], preferred_element_type=jnp.float32
    )
    pre_act = pre_act + proc_edge_bias[0]
    hidden = jax.nn.silu(pre_act).astype(jnp.bfloat16)
    edge_raw = lax.dot_general(
        hidden, piece_out, (((1,), (1,)), ((), ())), preferred_element_type=jnp.float32
    )
    edge_update = (
        mesh_edge.astype(jnp.float32) + layer_norm(edge_raw, proc_edge_gain, proc_edge_bias[1])
    ).astype(jnp.bfloat16)
    edge_onehot = (
        jnp.arange(mesh_rows, dtype=jnp.int32)[:, None] == mesh_receiver[None, :]
    ).astype(jnp.bfloat16)
    incoming = taken_together(
        jnp.dot(edge_onehot, edge_update, preferred_element_type=jnp.float32).astype(jnp.bfloat16),
        "lon",
    ).astype(jnp.float32)
    mesh_new = node_network(
        mesh_mid,
        incoming.astype(jnp.bfloat16),
        proc_node_in,
        proc_node_out,
        proc_node_bias,
        proc_node_gain,
    )
    mesh_update = lax.dynamic_slice_in_dim(mesh_new, lon_index * quarter, quarter, 1)
    return (mesh_update, edge_update)


def solution(mesh):
    placed = (
        P(("lat", "lon"), None),
        P(None, ("lat", "lon")),
        P(("lat", "lon")),
        P(("lat", "lon"), None),
        P(("lat", "lon")),
        P("lat", "lon"),
        P(("lat", "lon"), None),
        P("lat", None),
        P(("lat", "lon")),
        P(("lat", "lon")),
        P(None, "lon"),
        P(),
        P(None, "lon"),
        P(),
        P(),
        P(None, "lon"),
        P("lon", None),
        P(),
        P(),
        P(None, "lon"),
        P(None, "lon"),
        P(),
        P(),
        P(None, "lon"),
        P("lon", None),
        P(),
        P(),
    )
    return jax.shard_map(
        local,
        mesh=mesh,
        in_specs=placed,
        out_specs=(P("lat", "lon"), P(("lat", "lon"), None)),
        check_vma=False,
    )
```

profile of v0, /device:TPU:1, one launch (start us, length us, event | category | flops | bytes accessed | tf_op | source)
XLA Modules:
  0.0 435.4 jit_solution(5968562164946990583)
XLA Ops:
  7.2 1.7 pad_maximum_fusion.2
  9.0 0.8 fusion.33
  9.8 18.1 %reduce-window.6 = s32[64,16,128]{2,1,0:T(8,128)S(1)} reduce-window(s32[64,16,128]{2,1,0:T(8,128)S(1)} %fusion.33, s32[]{:T(128)} %constant.23.clone.1), window={size=1x1x128 pad=0_0x0_0x127_0}, to_apply=%region_0.0 | reduce-window | flops 16646144 | bytes 1048580 | tf_op jit(solution)/shard_map/reduce-window
  29.3 8.2 %scatter_custom_fusion = s32[4096]{0:T(1024)S(1)} fusion(s32[2048]{0:T(1024)S(1)} %bitcast.83, s32[2048]{0:T(1024)} %param.31, s32[]{:T(128)} %constant.21.clone.1), kind=kCustom, calls=%fused_computation.88 | custom fusion | bytes 16896 | tf_op jit(solution)/shard_map/scatter | solution.py:114
  38.2 15.1 %all-to-all-start.1 = ((s32[64,1,64]{2,1,0:T(1,128)}), s32[64,1,64]{2,1,0:T(1,128)S(1)}, u32[]{:S(2)}, u32[]{:S(2)}) async-start(s32[64,1,64]{2,1,0:T(1,128)} %all_to_all.28), calls=%async_computation.1 | async-start | bytes 65536 | tf_op jit(solution)/shard_map/all_to_all | solution.py:136
  53.4 7.5 %gather_fusion = bf16[2048,512]{1,0:T(8,128)(2,1)S(1)} fusion(bf16[512,512]{1,0:T(8,128)(2,1)S(1)} %copy-done, s32[2048]{0:T(1024)S(1)} %fusion.50), kind=kCustom, calls=%fused_computation | custom fusion | bytes 4202496 | tf_op jit(solution)/shard_map/gather | solution.py:117
  61.0 4.2 fusion.31
  65.2 6.6 %fusion.69 = (f32[2048]{0:T(1024)S(1)}, f32[2048,512]{0,1:T(8,128)}) fusion(bf16[1024,512]{1,0:T(8,128)(2,1)} %all-gather.3.cloned.1.call-done, f32[2048,512]{1,0:T(8,128)} %fusion.31, bf16[4,2048]{1,0:T(4,128)(2,1)S(1)} %copy-done.25, bf16[4,512]{1,0:T(4,128)(2,1)S(1)} %copy-done.26, f32[512]{0:T(512)S(1)} %bitcast.89), kind=kOutput, calls=%fused_computation.114 | convolution fusion | flops 1090516992 | bytes 8943616 | tf_op jit(solution)/shard_map/dot_general | solution.py:48
  71.9 2.8 multiply_reduce_fusion
  75.3 2.6 multiply_add_fusion
  77.9 5.3 %copy.53 = f32[2048,512]{1,0:T(8,128)} copy(f32[2048,512]{0,1:T(8,128)} %multiply_add_fusion) | data formatting | bytes 8388608 | tf_op jit(solution)/shard_map/add | solution.py:40
  83.3 13.4 %scatter_custom_fusion.1 = f32[4096,512]{1,0:T(8,128)} fusion(s32[2048]{0:T(1024)S(1)} %bitcast.84, f32[2048,512]{1,0:T(8,128)} %copy.53, f32[]{:T(128)} %constant.20.clone.1), kind=kCustom, calls=%fused_computation.16 | custom fusion | bytes 8389120 | tf_op jit(solution)/shard_map/scatter | solution.py:129
  96.6 5.9 %convert_element_type.69 = bf16[4096,512]{1,0:T(8,128)(2,1)} convert(f32[4096,512]{1,0:T(8,128)} %scatter_custom_fusion.1) | non-fusion elementwise | flops 2097152 | bytes 12582912 | tf_op jit(solution)/shard_map/convert_element_type | solution.py:134
  102.5 12.6 %all-to-all-start.2 = ((bf16[64,64,512]{2,1,0:T(8,128)(2,1)}), bf16[64,64,512]{2,1,0:T(8,128)(2,1)}, u32[]{:S(2)}, u32[]{:S(2)}) async-start(bf16[64,64,512]{2,1,0:T(8,128)(2,1)} %bitcast.73), calls=%async_computation.2 | async-start | bytes 8388608 | tf_op jit(solution)/shard_map/all_to_all | solution.py:133
  116.4 90.3 %all-to-all-done.2 = bf16[64,64,512]{2,1,0:T(8,128)(2,1)} async-done(((bf16[64,64,512]{2,1,0:T(8,128)(2,1)}), bf16[64,64,512]{2,1,0:T(8,128)(2,1)}, u32[]{:S(2)}, u32[]{:S(2)}) %all-to-all-start.2) | async-done | bytes 4194336 | tf_op jit(solution)/shard_map/all_to_all | solution.py:133
  206.7 0.9 broadcast_in_dim.28
  207.6 8.4 %all-to-all-start = ((bf16[4,512,128]{2,1,0:T(8,128)(2,1)}), bf16[4,512,128]{2,1,0:T(8,128)(2,1)S(1)}, u32[]{:S(2)}, u32[]{:S(2)}) async-start(bf16[4,512,128]{2,1,0:T(8,128)(2,1)} %broadcast_in_dim.28), calls=%async_computation | async-start | bytes 1048576 | tf_op jit(solution)/shard_map/all_to_all | solution.py:18
  216.0 28.1 %scatter_custom_fusion.2 = f32[513,512]{1,0:T(8,128)S(1)} fusion(s32[4096]{0:T(1024)S(1)} %bitcast.81, bf16[4096,512]{1,0:T(8,128)(2,1)} %bitcast.22, f32[]{:T(128)} %constant.20.clone.1), kind=kCustom, calls=%fused_computation.7 | custom fusion | flops 4194304 | bytes 5244932 | tf_op jit(solution)/shard_map/scatter-add | solution.py:141
  244.3 1.5 broadcast_in_dim.66
  245.8 3.7 all-to-all-start.3
  249.6 24.7 %all-to-all-done.3 = bf16[4,512,512]{2,1,0:T(8,128)(2,1)S(1)} async-done(((bf16[4,512,512]{2,1,0:T(8,128)(2,1)}), bf16[4,512,512]{2,1,0:T(8,128)(2,1)S(1)}, u32[]{:S(2)}, u32[]{:S(2)}) %all-to-all-start.3) | async-done | bytes 2097184 | tf_op jit(solution)/shard_map/all_to_all | solution.py:18
  274.3 1.2 reduce_sum.129
  275.5 1.6 convolution_convert_fusion.1
  277.2 1.5 broadcast_in_dim.67
  278.6 4.6 %all-to-all-start.4 = ((bf16[4,512,512]{2,1,0:T(8,128)(2,1)}), bf16[4,512,512]{2,1,0:T(8,128)(2,1)S(1)}, u32[]{:S(2)}, u32[]{:S(2)}) async-start(bf16[4,512,512]{2,1,0:T(8,128)(2,1)} %broadcast_in_dim.67), calls=%async_computation.4 | async-start | bytes 4194304 | tf_op jit(solution)/shard_map/all_to_all | solution.py:18
  283.3 0.8 pad_maximum_fusion.1
  284.4 33.2 %all-to-all-done.4 = bf16[4,512,512]{2,1,0:T(8,128)(2,1)S(1)} async-done(((bf16[4,512,512]{2,1,0:T(8,128)(2,1)}), bf16[4,512,512]{2,1,0:T(8,128)(2,1)S(1)}, u32[]{:S(2)}, u32[]{:S(2)}) %all-to-all-start.4) | async-done | bytes 2097184 | tf_op jit(solution)/shard_map/all_to_all | solution.py:18
  318.7 2.6 gather_fusion.1
  321.3 6.8 %all-to-all-start.5 = ((bf16[64,8,512]{2,1,0:T(8,128)(2,1)}), bf16[64,8,512]{2,1,0:T(8,128)(2,1)S(1)}, u32[]{:S(2)}, u32[]{:S(2)}) async-start(bf16[64,8,512]{2,1,0:T(8,128)(2,1)} %bitcast.16), calls=%async_computation.5 | async-start | bytes 1048576 | tf_op jit(solution)/shard_map/all_to_all | solution.py:153
  328.1 1.3 copy.54
  329.5 4.0 gather_fusion.3
  333.5 3.1 fusion.23
  336.6 6.8 %all-to-all-done.5 = bf16[64,8,512]{2,1,0:T(8,128)(2,1)S(1)} async-done(((bf16[64,8,512]{2,1,0:T(8,128)(2,1)}), bf16[64,8,512]{2,1,0:T(8,128)(2,1)S(1)}, u32[]{:S(2)}, u32[]{:S(2)}) %all-to-all-start.5) | async-done | bytes 524320 | tf_op jit(solution)/shard_map/all_to_all | solution.py:153
  343.5 4.0 gather_fusion.2
  347.5 3.1 fusion.25
  350.6 4.5 %fusion.70 = (f32[1024]{0:T(1024)S(1)}, f32[1024,512]{0,1:T(8,128)S(1)}) fusion(f32[1024,512]{0,1:T(8,128)} %fusion.23, f32[1024,512]{0,1:T(8,128)} %fusion.25, bf16[1024,512]{1,0:T(8,128)(2,1)} %param.33, f32[512]{0:T(512)S(1)} %bitcast.87, bf16[2048,512]{1,0:T(8,128)(2,1)} %all-gather.5.cloned.1.call-done), kind=kOutput, calls=%fused_computation.115 | convolution fusion | flops 1078459392 | bytes 8394752 | tf_op jit(solution)/shard_map/dot_general | solution.py:167
  355.5 0.9 copy-done.4
  356.9 1.0 copy-done.3
  358.6 1.5 broadcast_in_dim.71
  360.1 8.5 %all-to-all-start.6 = ((bf16[4,512,512]{2,1,0:T(8,128)(2,1)}), bf16[4,512,512]{2,1,0:T(8,128)(2,1)S(1)}, u32[]{:S(2)}, u32[]{:S(2)}) async-start(bf16[4,512,512]{2,1,0:T(8,128)(2,1)} %broadcast_in_dim.71), calls=%async_computation.6 | async-start | bytes 4194304 | tf_op jit(solution)/shard_map/all_to_all | solution.py:18
  368.7 24.7 %all-to-all-done.6 = bf16[4,512,512]{2,1,0:T(8,128)(2,1)S(1)} async-done(((bf16[4,512,512]{2,1,0:T(8,128)(2,1)}), bf16[4,512,512]{2,1,0:T(8,128)(2,1)S(1)}, u32[]{:S(2)}, u32[]{:S(2)}) %all-to-all-start.6) | async-done | bytes 2097184 | tf_op jit(solution)/shard_map/all_to_all | solution.py:18
  393.4 1.2 reduce_sum.135
  394.6 1.6 convolution_convert_fusion
  396.3 1.5 broadcast_in_dim.72
  397.8 4.5 %all-to-all-start.7 = ((bf16[4,512,512]{2,1,0:T(8,128)(2,1)}), bf16[4,512,512]{2,1,0:T(8,128)(2,1)S(1)}, u32[]{:S(2)}, u32[]{:S(2)}) async-start(bf16[4,512,512]{2,1,0:T(8,128)(2,1)} %broadcast_in_dim.72), calls=%async_computation.7 | async-start | bytes 4194304 | tf_op jit(solution)/shard_map/all_to_all | solution.py:18
  403.1 2.3 copy.58
  405.4 21.6 %all-to-all-done.7 = bf16[4,512,512]{2,1,0:T(8,128)(2,1)S(1)} async-done(((bf16[4,512,512]{2,1,0:T(8,128)(2,1)}), bf16[4,512,512]{2,1,0:T(8,128)(2,1)S(1)}, u32[]{:S(2)}, u32[]{:S(2)}) %all-to-all-start.7) | async-done | bytes 2097184 | tf_op jit(solution)/shard_map/all_to_all | solution.py:18
  427.8 0.8 fusion.37
  (105 shorter events, 8.9 us)
Async XLA Ops:
  7.2 46.2 %copy-start = (bf16[512,512]{1,0:T(8,128)(2,1)S(1)}, bf16[512,512]{1,0:T(8,128)(2,1)}, u32[]{:S(2)}) copy-start(bf16[512,512]{1,0:T(8,128)(2,1)} %param.27) | copy-start | bytes 1572868
  7.2 53.8 %all-gather.3.cloned.1.call-start = ((), (), s32[]{:S(2)}) async-start(), calls=%async_computation.8 | async-start | bytes 1310720 | tf_op jit(solution)/shard_map/all_gather | solution.py:9
  9.0 20.0 %copy-start.9 = (s32[2048,1]{0,1:T(1,128)S(1)}, s32[2048,1]{0,1:T(1,128)}, u32[]{:S(2)}) copy-start(s32[2048,1]{0,1:T(1,128)} %param.30) | copy-start | bytes 24580
  9.8 43.5 %copy-start.10 = (s32[2048]{0:T(1024)S(1)}, s32[2048]{0:T(1024)}, u32[]{:S(2)}) copy-start(s32[2048]{0:T(1024)} %param.29) | copy-start | bytes 24580
  38.2 64.3 %all-to-all-start.1 = ((s32[64,1,64]{2,1,0:T(1,128)}), s32[64,1,64]{2,1,0:T(1,128)S(1)}, u32[]{:S(2)}, u32[]{:S(2)}) async-start(s32[64,1,64]{2,1,0:T(1,128)} %all_to_all.28), calls=%async_computation.1 | async-start | bytes 65536 | tf_op jit(solution)/shard_map/all_to_all | solution.py:136
  53.4 7.6 %copy-start.11 = (f32[2,512]{1,0:T(2,128)S(1)}, f32[2,512]{1,0:T(2,128)}, u32[]{:S(2)}) copy-start(f32[2,512]{1,0:T(2,128)} %param.40) | copy-start | bytes 12292
  61.0 4.3 copy-start.25
  61.0 4.3 copy-start.26
  71.9 3.4 copy-start.2
  71.9 3.4 copy-start.20
  102.5 104.2 %copy-start.7 = (bf16[512,128]{1,0:T(8,128)(2,1)S(1)}, bf16[512,128]{1,0:T(8,128)(2,1)}, u32[]{:S(2)}) copy-start(bf16[512,128]{1,0:T(8,128)(2,1)} %param.32) | copy-start | bytes 393220
  102.5 104.2 %all-to-all-start.2 = ((bf16[64,64,512]{2,1,0:T(8,128)(2,1)}), bf16[64,64,512]{2,1,0:T(8,128)(2,1)}, u32[]{:S(2)}, u32[]{:S(2)}) async-start(bf16[64,64,512]{2,1,0:T(8,128)(2,1)} %bitcast.73), calls=%async_computation.2 | async-start | bytes 8388608 | tf_op jit(solution)/shard_map/all_to_all | solution.py:133
  207.6 36.7 %all-to-all-start = ((bf16[4,512,128]{2,1,0:T(8,128)(2,1)}), bf16[4,512,128]{2,1,0:T(8,128)(2,1)S(1)}, u32[]{:S(2)}, u32[]{:S(2)}) async-start(bf16[4,512,128]{2,1,0:T(8,128)(2,1)} %broadcast_in_dim.28), calls=%async_computation | async-start | bytes 1048576 | tf_op jit(solution)/shard_map/all_to_all | solution.py:18
  245.8 3.8 copy-start.12
  245.8 28.5 %all-to-all-start.3 = ((bf16[4,512,512]{2,1,0:T(8,128)(2,1)}), bf16[4,512,512]{2,1,0:T(8,128)(2,1)S(1)}, u32[]{:S(2)}, u32[]{:S(2)}) async-start(bf16[4,512,512]{2,1,0:T(8,128)(2,1)} %broadcast_in_dim.66), calls=%async_computation.3 | async-start | bytes 4194304 | tf_op jit(solution)/shard_map/all_to_all | solution.py:18
  249.5 26.0 %copy-start.21 = (bf16[1024,128]{1,0:T(8,128)(2,1)S(1)}, bf16[1024,128]{1,0:T(8,128)(2,1)}, u32[]{:S(2)}) copy-start(bf16[1024,128]{1,0:T(8,128)(2,1)} %param.42) | copy-start | bytes 786436
  249.5 26.0 %copy-start.23 = (bf16[128,512]{1,0:T(8,128)(2,1)S(1)}, bf16[128,512]{1,0:T(8,128)(2,1)}, u32[]{:S(2)}) copy-start(bf16[128,512]{1,0:T(8,128)(2,1)} %param.43) | copy-start | bytes 393220
  278.6 4.6 %copy-start.6 = (bf16[1536,128]{1,0:T(8,128)(2,1)S(1)}, bf16[1536,128]{1,0:T(8,128)(2,1)}, u32[]{:S(2)}) copy-start(bf16[1536,128]{1,0:T(8,128)(2,1)} %param.46) | copy-start | bytes 1179652
  278.6 4.6 %copy-start.8 = (bf16[512,128]{1,0:T(8,128)(2,1)S(1)}, bf16[512,128]{1,0:T(8,128)(2,1)}, u32[]{:S(2)}) copy-start(bf16[512,128]{1,0:T(8,128)(2,1)} %param.47) | copy-start | bytes 393220
  278.6 5.5 %copy-start.13 = (s32[64,8]{0,1:T(8,128)S(1)}, s32[64,8]{0,1:T(8,128)}, u32[]{:S(2)}) copy-start(s32[64,8]{0,1:T(8,128)} %param.34) | copy-start | bytes 6148
  278.6 39.0 %all-to-all-start.4 = ((bf16[4,512,512]{2,1,0:T(8,128)(2,1)}), bf16[4,512,512]{2,1,0:T(8,128)(2,1)S(1)}, u32[]{:S(2)}, u32[]{:S(2)}) async-start(bf16[4,512,512]{2,1,0:T(8,128)(2,1)} %broadcast_in_dim.67), calls=%async_computation.4 | async-start | bytes 4194304 | tf_op jit(solution)/shard_map/all_to_all | solution.py:18
  283.3 50.2 %all-gather.5.cloned.1.call-start = ((), (), s32[]{:S(2)}) async-start(), calls=%async_computation.9 | async-start | bytes 2621440 | tf_op jit(solution)/shard_map/all_gather | solution.py:9
  284.4 34.0 %copy-start.19 = (f32[512]{0:T(512)S(1)}, f32[512]{0:T(512)}, u32[]{:S(2)}) copy-start(f32[512]{0:T(512)} %param.45) | copy-start | bytes 6148
  318.7 9.5 %copy-start.5 = (bf16[1024,512]{1,0:T(8,128)(2,1)S(1)}, bf16[1024,512]{1,0:T(8,128)(2,1)}, u32[]{:S(2)}) copy-start(bf16[1024,512]{1,0:T(8,128)(2,1)} %param.33) | copy-start | bytes 3145732
  321.3 8.1 %copy-start.14 = (s32[1024]{0:T(1024)S(1)}, s32[1024]{0:T(1024)}, u32[]{:S(2)}) copy-start(s32[1024]{0:T(1024)} %param.35) | copy-start | bytes 12292
  321.3 8.1 %copy-start.16 = (s32[1024]{0:T(1024)S(1)}, s32[1024]{0:T(1024)}, u32[]{:S(2)}) copy-start(s32[1024]{0:T(1024)} %param.36) | copy-start | bytes 12292
  321.3 8.2 %copy-start.15 = (f32[2,512]{1,0:T(2,128)S(1)}, f32[2,512]{1,0:T(2,128)}, u32[]{:S(2)}) copy-start(f32[2,512]{1,0:T(2,128)} %param.48) | copy-start | bytes 12292
  321.3 22.1 %all-to-all-start.5 = ((bf16[64,8,512]{2,1,0:T(8,128)(2,1)}), bf16[64,8,512]{2,1,0:T(8,128)(2,1)S(1)}, u32[]{:S(2)}, u32[]{:S(2)}) async-start(bf16[64,8,512]{2,1,0:T(8,128)(2,1)} %bitcast.16), calls=%async_computation.5 | async-start | bytes 1048576 | tf_op jit(solution)/shard_map/all_to_all | solution.py:153
  355.1 1.2 copy-start.4
  355.2 1.2 copy-start.18
  356.9 1.0 copy-start.3
  360.1 8.6 %copy-start.17 = (f32[2,512]{1,0:T(2,128)S(1)}, f32[2,512]{1,0:T(2,128)}, u32[]{:S(2)}) copy-start(f32[2,512]{1,0:T(2,128)} %param.52) | copy-start | bytes 12292
  360.1 33.3 %all-to-all-start.6 = ((bf16[4,512,512]{2,1,0:T(8,128)(2,1)}), bf16[4,512,512]{2,1,0:T(8,128)(2,1)S(1)}, u32[]{:S(2)}, u32[]{:S(2)}) async-start(bf16[4,512,512]{2,1,0:T(8,128)(2,1)} %broadcast_in_dim.71), calls=%async_computation.6 | async-start | bytes 4194304 | tf_op jit(solution)/shard_map/all_to_all | solution.py:18
  368.7 25.9 %copy-start.22 = (bf16[1024,128]{1,0:T(8,128)(2,1)S(1)}, bf16[1024,128]{1,0:T(8,128)(2,1)}, u32[]{:S(2)}) copy-start(bf16[1024,128]{1,0:T(8,128)(2,1)} %param.50) | copy-start | bytes 786436
  368.7 25.9 %copy-start.24 = (bf16[128,512]{1,0:T(8,128)(2,1)S(1)}, bf16[128,512]{1,0:T(8,128)(2,1)}, u32[]{:S(2)}) copy-start(bf16[128,512]{1,0:T(8,128)(2,1)} %param.51) | copy-start | bytes 393220
  397.8 29.2 %all-to-all-start.7 = ((bf16[4,512,512]{2,1,0:T(8,128)(2,1)}), bf16[4,512,512]{2,1,0:T(8,128)(2,1)S(1)}, u32[]{:S(2)}, u32[]{:S(2)}) async-start(bf16[4,512,512]{2,1,0:T(8,128)(2,1)} %broadcast_in_dim.72), calls=%async_computation.7 | async-start | bytes 4194304 | tf_op jit(solution)/shard_map/all_to_all | solution.py:18
  427.0 1.6 copy-start.1
Sparse Core Ops, SparseCore 0:
  10.4 27.0 all-gather.2
  285.9 39.4 all-gather.4
where the time goes:
time: 437 us; the launch traced here: 435 us
  waiting for transfers between devices  201 us (46%)
  other arithmetic  68.3 us (16%)
  starting transfers between devices  64.4 us (15%)
  local copies, waits for them, and re-layouts  61.2 us (14%)
  matrix products  25.6 us (6%)
  between operations  14.5 us (3%)
    all_to_all x5, waiting for transfers between devices, sent_to_all(): return lax.all_to_all(copies, axis, split_axis=0, concat_axis=0, tiled=True)  104 us
    all_to_all x1, waiting for transfers between devices, local(): lax.all_to_all(buffer.astype(jnp.bfloat16), 'lat', split_axis=0, concat_a...  90.3 us
    all_to_all x5, starting transfers between devices, sent_to_all(): return lax.all_to_all(copies, axis, split_axis=0, concat_axis=0, tiled=True)  29.9 us
    scatter-add x1, other arithmetic, local(): jax.ops.segment_sum(arrived, segment_ids, num_segments=mesh_rows + 1)  28.1 us
    another operation x3, other arithmetic  18.5 us
    all_to_all x1, starting transfers between devices, local(): lax.all_to_all(node_slots, 'lat', split_axis=0, concat_axis=0, tiled=True)  15.1 us
    scatter x1, local copies, waits for them, and re-layouts, local(): buffer = jnp.zeros((slot_total, feature_width), jnp.float32).at[slot_inde...  13.4 us
    all_to_all x1, starting transfers between devices, local(): lax.all_to_all(buffer.astype(jnp.bfloat16), 'lat', split_axis=0, concat_a...  12.6 us
  transfers between devices with their start and end apart: 10, of which 6 were waited for; matrix products, arithmetic and copies ran while one was open for 28% of the time, Pallas kernels for 0%

commit v1 on v0

v1 whole, which is shorter than its diff:
```python
import jax
import jax.numpy as jnp
from jax import lax
from jax.experimental import pallas as pl
from jax.experimental.pallas import tpu as pltpu
from jax.sharding import PartitionSpec as P

F32 = jnp.float32
BF16 = jnp.bfloat16
LAT = 64
LON = 4
WIDTH = 512
NODES = 512
CAP = 64
ROWS = NODES // LON


def matmul(a, b):
    return jnp.dot(a, b, preferred_element_type=F32)


def matmul_t(a, b):
    return lax.dot_general(a, b, (((0,), (0,)), ((), ())), preferred_element_type=F32)


def matmul_nt(a, b):
    return lax.dot_general(a, b, (((1,), (1,)), ((), ())), preferred_element_type=F32)


def swish(t):
    return t / (1.0 + jnp.exp(-t))


def layer_norm(values, gain, offset):
    average = jnp.mean(values, axis=-1, keepdims=True)
    centred = values - average
    spread = jnp.mean(centred * centred, axis=-1, keepdims=True)
    return centred * lax.rsqrt(spread + 1e-05) * gain + offset


def one_hot(row, count):
    width = row.shape[1]
    return (lax.broadcasted_iota(jnp.int32, (count, width), 0) == row).astype(BF16)


def slot_fields(owners, sender, node, feat):
    count = owners.shape[0]
    block = 128
    hit = (owners[:, None] == jnp.arange(LAT, dtype=jnp.int32)[None, :]).astype(BF16)
    blocks = hit.reshape(count // block, block, LAT)
    below = jnp.tril(jnp.ones((block, block), BF16), -1)
    inside = jnp.einsum("ij,bjk->bik", below, blocks, preferred_element_type=F32)
    totals = jnp.sum(blocks.astype(F32), axis=1)
    earlier = jnp.tril(jnp.ones((count // block, count // block), F32), -1)
    before = jnp.sum(earlier[:, :, None] * totals[None], axis=1)
    rank = jnp.sum((inside + before[:, None, :]) * blocks.astype(F32), axis=2).reshape(count)
    place = (rank.astype(jnp.int32)[:, None] == jnp.arange(CAP, dtype=jnp.int32)[None, :]).astype(BF16)
    shifted = node + 1
    values = [sender >> 8, sender & 255, shifted >> 8, shifted & 255]
    values = [v.astype(BF16) for v in values] + [feat[i] for i in range(4)]
    spread = jnp.concatenate([place * v[:, None] for v in values], axis=1)
    slots = matmul_t(hit, spread).reshape(LAT, 8, CAP)
    return jnp.moveaxis(slots, 1, 0).reshape(8, LAT * CAP)


def encoder_kernel(step, sender, feat, grid, w_in, proj, w_out, bias, gain, out):
    rows = matmul_t(one_hot(sender[...], WIDTH), grid[...]).astype(BF16)
    pre = matmul(rows, w_in[...]) + (matmul_t(feat[...], proj[...]) + bias[0:1, :])
    hidden = swish(pre).astype(BF16)
    raw = matmul_nt(hidden, w_out[...])
    out[...] = layer_norm(raw, gain[...], bias[1:2, :]).astype(BF16)


def encode(sender, feat, grid, w_in, proj, w_out, bias, gain):
    total = sender.shape[1]
    step = 256
    whole = lambda i: (0, 0)
    return pl.pallas_call(
        lambda *refs: encoder_kernel(step, *refs),
        grid=(total // step,),
        in_specs=[
            pl.BlockSpec((1, step), lambda i: (0, i)),
            pl.BlockSpec((8, step), lambda i: (0, i)),
            pl.BlockSpec((512, WIDTH), whole),
            pl.BlockSpec((WIDTH, WIDTH), whole),
            pl.BlockSpec((8, WIDTH), whole),
            pl.BlockSpec((WIDTH, WIDTH), whole),
            pl.BlockSpec((2, WIDTH), whole),
            pl.BlockSpec((1, WIDTH), whole),
        ],
        out_specs=pl.BlockSpec((step, WIDTH), lambda i: (i, 0)),
        out_shape=jax.ShapeDtypeStruct((total, WIDTH), BF16),
        name="encode",
    )(sender, feat, grid, w_in, proj, w_out, bias, gain)


def segment_kernel(ids, rows, out, acc):
    @pl.when(pl.program_id(0) == 0)
    def _():
        acc[...] = jnp.zeros_like(acc)

    acc[...] += matmul(one_hot(ids[...], NODES), rows[...])

    @pl.when(pl.program_id(0) == pl.num_programs(0) - 1)
    def _():
        out[...] = acc[...].astype(BF16)


def segment_sum(ids, rows):
    total = rows.shape[0]
    step = 512
    return pl.pallas_call(
        segment_kernel,
        grid=(total // step,),
        in_specs=[
            pl.BlockSpec((1, step), lambda i: (0, i)),
            pl.BlockSpec((step, WIDTH), lambda i: (i, 0)),
        ],
        out_specs=pl.BlockSpec((NODES, WIDTH), lambda i: (0, 0)),
        out_shape=jax.ShapeDtypeStruct((NODES, WIDTH), BF16),
        scratch_shapes=[pltpu.VMEM((NODES, WIDTH), F32)],
        name="segment",
    )(ids, rows)


def node_kernel(base, parts, w_in, w_out, bias, gain, out):
    summed = parts[0].astype(F32)
    for i in range(1, LON):
        summed = summed + parts[i].astype(F32)
    aggregate = summed.astype(BF16)
    pre = matmul(base[...], w_in[:WIDTH, :]) + matmul(aggregate, w_in[WIDTH:, :]) + bias[0:1, :]
    hidden = swish(pre).astype(BF16)
    raw = matmul(hidden, w_out[...])
    out[...] = (base[...].astype(F32) + layer_norm(raw, gain[...], bias[1:2, :])).astype(BF16)


def node_network(base, parts, w_in, w_out, bias, gain):
    return pl.pallas_call(
        node_kernel, out_shape=jax.ShapeDtypeStruct(base.shape, BF16), name="node"
    )(base, parts, w_in, w_out, bias, gain)


def edge_kernel(sender, receiver, edges, local, halo, w_in, w_out, bias, gain, out, partial, acc):
    @pl.when(pl.program_id(0) == 0)
    def _():
        acc[...] = jnp.zeros_like(acc)

    towards = one_hot(receiver[...], NODES)
    sent = matmul_t(one_hot(sender[...], NODES), local[...])
    sent = sent + matmul_t(one_hot(sender[...] - NODES, NODES), halo[...])
    got = matmul_t(towards, local[...])
    pre = matmul(edges[...], w_in[:WIDTH, :])
    pre = pre + matmul(sent.astype(BF16), w_in[WIDTH : 2 * WIDTH, :])
    pre = pre + matmul(got.astype(BF16), w_in[2 * WIDTH :, :])
    hidden = swish(pre + bias[0:1, :]).astype(BF16)
    raw = matmul_nt(hidden, w_out[...])
    updated = (edges[...].astype(F32) + layer_norm(raw, gain[...], bias[1:2, :])).astype(BF16)
    out[...] = updated
    acc[...] += matmul(towards, updated)

    @pl.when(pl.program_id(0) == pl.num_programs(0) - 1)
    def _():
        partial[...] = acc[...].astype(BF16)


def edge_network(sender, receiver, edges, local, halo, w_in, w_out, bias, gain):
    total = edges.shape[0]
    step = 256
    whole = lambda i: (0, 0)
    return pl.pallas_call(
        edge_kernel,
        grid=(total // step,),
        in_specs=[
            pl.BlockSpec((1, step), lambda i: (0, i)),
            pl.BlockSpec((1, step), lambda i: (0, i)),
            pl.BlockSpec((step, WIDTH), lambda i: (i, 0)),
            pl.BlockSpec((NODES, WIDTH), whole),
            pl.BlockSpec((NODES, WIDTH), whole),
            pl.BlockSpec((3 * WIDTH, WIDTH), whole),
            pl.BlockSpec((WIDTH, WIDTH), whole),
            pl.BlockSpec((2, WIDTH), whole),
            pl.BlockSpec((1, WIDTH), whole),
        ],
        out_specs=[
            pl.BlockSpec((step, WIDTH), lambda i: (i, 0)),
            pl.BlockSpec((NODES, WIDTH), whole),
        ],
        out_shape=[
            jax.ShapeDtypeStruct((total, WIDTH), BF16),
            jax.ShapeDtypeStruct((NODES, WIDTH), BF16),
        ],
        scratch_shapes=[pltpu.VMEM((NODES, WIDTH), F32)],
        name="edges",
    )(sender, receiver, edges, local, halo, w_in, w_out, bias, gain)


def swap(tiles, axis):
    return lax.all_to_all(tiles, axis, split_axis=0, concat_axis=0, tiled=True)


def local(
    grid_latent,
    grid_feat,
    grid_sender,
    grid_owner,
    grid_node,
    mesh_latent,
    mesh_edge,
    halo_send,
    mesh_sender,
    mesh_receiver,
    enc_edge_in,
    enc_feat_proj,
    enc_edge_out,
    enc_edge_bias,
    enc_edge_gain,
    enc_node_in,
    enc_node_out,
    enc_node_bias,
    enc_node_gain,
    proc_edge_in,
    proc_edge_out,
    proc_edge_bias,
    proc_edge_gain,
    proc_node_in,
    proc_node_out,
    proc_node_bias,
    proc_node_gain,
):
    first = lax.all_gather(
        jnp.concatenate([enc_edge_in, enc_edge_out], 0), "lon", axis=1, tiled=True
    )
    inner = lax.all_gather(
        jnp.concatenate([enc_node_in, proc_edge_in, proc_edge_out, proc_node_in], 0),
        "lon",
        axis=1,
        tiled=True,
    )
    outer = lax.all_gather(
        jnp.concatenate([enc_node_out, proc_node_out], 1), "lon", axis=0, tiled=True
    )
    base = swap(mesh_latent.reshape(LON, ROWS, ROWS), "lon")
    base = jnp.moveaxis(base, 0, 1).reshape(ROWS, WIDTH)

    fields = slot_fields(grid_owner[:, 0], grid_sender, grid_node, grid_feat)
    whole = fields[:4].astype(jnp.int32)
    sender = (whole[0] * 256 + whole[1]).reshape(1, -1)
    node = (whole[2] * 256 + whole[3] - 1).reshape(LAT, 1, CAP)
    feat = jnp.concatenate([fields[4:], jnp.zeros((4, LAT * CAP), F32)], 0).astype(BF16)
    proj = jnp.concatenate([enc_feat_proj, jnp.zeros((4, WIDTH), BF16)], 0)
    ids = swap(node, "lat")
    messages = encode(
        sender, feat, grid_latent, first[:WIDTH], proj, first[WIDTH:], enc_edge_bias, enc_edge_gain[None]
    )
    arrived = swap(messages.reshape(LAT, CAP, WIDTH), "lat").reshape(LAT * CAP, WIDTH)
    partial = segment_sum(ids.reshape(1, LAT * CAP), arrived)
    parts = swap(partial.reshape(LON, ROWS, WIDTH), "lon")
    middle = node_network(
        base, parts, inner[:1024], outer[:, :WIDTH], enc_node_bias, enc_node_gain[None]
    )
    mesh_mid = lax.all_gather(middle, "lon", axis=0, tiled=True)
    halo = swap(mesh_mid[halo_send], "lat").reshape(NODES, WIDTH)
    edge_update, partial = edge_network(
        mesh_sender.reshape(1, -1),
        mesh_receiver.reshape(1, -1),
        mesh_edge,
        mesh_mid,
        halo,
        inner[1024:2560],
        inner[2560:3072],
        proc_edge_bias,
        proc_edge_gain[None],
    )
    parts = swap(partial.reshape(LON, ROWS, WIDTH), "lon")
    newest = node_network(
        middle, parts, inner[3072:], outer[:, WIDTH:], proc_node_bias, proc_node_gain[None]
    )
    tiles = jnp.moveaxis(newest.reshape(ROWS, LON, ROWS), 1, 0)
    mesh_update = swap(tiles, "lon").reshape(NODES, ROWS)
    return (mesh_update, edge_update)


def solution(mesh):
    placed = (
        P(("lat", "lon"), None),
        P(None, ("lat", "lon")),
        P(("lat", "lon")),
        P(("lat", "lon"), None),
        P(("lat", "lon")),
        P("lat", "lon"),
        P(("lat", "lon"), None),
        P("lat", None),
        P(("lat", "lon")),
        P(("lat", "lon")),
        P(None, "lon"),
        P(),
        P(None, "lon"),
        P(),
        P(),
        P(None, "lon"),
        P("lon", None),
        P(),
        P(),
        P(None, "lon"),
        P(None, "lon"),
        P(),
        P(),
        P(None, "lon"),
        P("lon", None),
        P(),
        P(),
    )
    return jax.shard_map(
        local,
        mesh=mesh,
        in_specs=placed,
        out_specs=(P("lat", "lon"), P(("lat", "lon"), None)),
        check_vma=False,
    )
```

time: 437 us -> 282 us (0.65)
  waiting for transfers between devices: 201 us -> 115 us
  other arithmetic: 68.3 us -> 11.4 us
  Pallas kernels: 0 us -> 42.4 us
  local copies, waits for them, and re-layouts: 61.2 us -> 28.5 us
  blocking collectives: 0 us -> 29.2 us
  starting transfers between devices: 64.4 us -> 38.8 us
  matrix products: 25.6 us -> 1.91 us
    all_to_all x8 -> x5, waiting for transfers between devices: 201 us -> 115 us  [swap(): return lax.all_to_all(tiles, axis, split_axis=0, concat_axis=0, tiled=True)]
    pallas_call x0 -> x5, Pallas kernels: none -> 42.4 us  [the longest x1 18.6 us: encode(): pl.pallas_call(lambda *refs: encoder_kernel(step, *refs), grid=(total //...]
    scatter-add x1 -> x0, other arithmetic: 28.1 us -> none  [local(): jax.ops.segment_sum(arrived, segment_ids, num_segments=mesh_rows + 1)]
    all_to_all x8 -> x5, starting transfers between devices: 64.3 us -> 38.7 us  [swap(): return lax.all_to_all(tiles, axis, split_axis=0, concat_axis=0, tiled=True)]
    dot_general x8 -> x2, matrix products: 25.6 us -> 1.91 us  [the longest x1 1.1 us: slot_fields(): jnp.einsum('ij,bjk->bik', below, blocks, preferred_element_type=F32)]
    all_to_all x0 -> x2, blocking collectives: none -> 21.7 us  [swap(): return lax.all_to_all(tiles, axis, split_axis=0, concat_axis=0, tiled=True)]
    scatter x2 -> x0, local copies, waits for them, and re-layouts: 21.6 us -> none  [the longest x1 13.4 us: local(): buffer = jnp.zeros((slot_total, feature_width), jnp.float32).at[slot_inde...]
    another operation x3 -> x0, other arithmetic: 18.5 us -> none
  transfers between devices with their start and end apart: 10 -> 8, of which waited for: 6 -> 4; matrix products, arithmetic and copies ran while one was open for 28% -> 12% of each run, Pallas kernels for 0% -> 9%
where the time goes in v1:
time: 282 us; the launch traced here: 281 us
  waiting for transfers between devices  115 us (41%)
  Pallas kernels  42.4 us (15%)
  starting transfers between devices  38.8 us (14%)
  blocking collectives  29.2 us (10%)
  local copies, waits for them, and re-layouts  28.5 us (10%)
  between operations  14 us (5%)
  other arithmetic  11.4 us (4%)
    all_to_all x5, waiting for transfers between devices, swap(): return lax.all_to_all(tiles, axis, split_axis=0, concat_axis=0, tiled=True)  115 us
    all_to_all x5, starting transfers between devices, swap(): return lax.all_to_all(tiles, axis, split_axis=0, concat_axis=0, tiled=True)  38.7 us
    all_to_all x2, blocking collectives, swap(): return lax.all_to_all(tiles, axis, split_axis=0, concat_axis=0, tiled=True)  21.7 us
    pallas_call x1, Pallas kernels, encode(): pl.pallas_call(lambda *refs: encoder_kernel(step, *refs), grid=(total //...  18.6 us
    pallas_call x1, Pallas kernels, edge_network(): pl.pallas_call(edge_kernel, grid=(total // step,), in_specs=[pl.BlockSpec...  10.4 us
    all_gather x1, blocking collectives, local(): mesh_mid = lax.all_gather(middle, 'lon', axis=0, tiled=True)  7.51 us
    pallas_call x1, Pallas kernels, segment_sum(): pl.pallas_call(segment_kernel, grid=(total // step,), in_specs=[pl.BlockS...  7.46 us
    pallas_call x2, Pallas kernels, node_network(): pl.pallas_call(node_kernel, out_shape=jax.ShapeDtypeStruct(base.shape, BF...  5.92 us
  transfers between devices with their start and end apart: 8, of which 4 were waited for; matrix products, arithmetic and copies ran while one was open for 12% of the time, Pallas kernels for 9%

profile of v1, /device:TPU:1, one launch (start us, length us, event | category | flops | bytes accessed | tf_op | source)
XLA Modules:
  0.0 280.9 jit_solution(3219415739733148256)
XLA Ops:
  7.2 1.7 pad_maximum_fusion.1
  9.0 0.9 convert_reduce_fusion
  9.9 0.1 multiply_reduce_fusion
  10.1 1.1 fusion.2
  11.2 1.0 slice_reduce_fusion
  12.1 0.7 and_convert_fusion
  12.9 4.7 %fusion.3 = (bf16[2048,64]{1,0:T(8,128)(2,1)S(1)}, bf16[2048,64]{1,0:T(8,128)(2,1)S(1)}, bf16[2048,64]{1,0:T(8,128)(2,1)}, bf16[2048,64]{1,0:T(8,128)(2,1)}, bf1...) fusion(s32[2048]{0:T(1024)S(1)} %convert_bitcast_fusion, ...), kind=kLoop, calls=%fused_computation.7 | loop fusion | flops 1179648 | bytes 2138112 | tf_op jit(solution)/shard_map/mul | solution.py:61
  17.6 5.3 %concatenate.18 = bf16[2048,512]{1,0:T(8,128)(2,1)S(1)} concatenate(bf16[2048,64]{1,0:T(8,128)(2,1)} %get-tuple-element.25, bf16[2048,64]{1,0:T(8,128)(2,1)} %get-tuple-element.24, bf16[2048,64]{1,0:T(8,128)(2,1)} %get-tuple-element.23, bf16[2048,64]{1,0:T(8,128)(2,1)} %get-tuple-element.22, bf16[2048,64]{1,0:T(8,128)(2,1)} %get-tuple-element.21, ...), dimensions={1} | concatenate | bytes 4194304 | tf_op jit(solution)/shard_map/concatenate | solution.py:61
  22.9 0.8 fusion.11
  23.7 0.1 reshape.143
  23.9 0.6 slice_add_fusion
  24.6 15.1 %all-to-all-start.1 = ((s32[64,1,64]{2,1,0:T(1,128)}), s32[64,1,64]{2,1,0:T(1,128)S(1)}, u32[]{:S(2)}, u32[]{:S(2)}) async-start(s32[64,1,64]{2,1,0:T(1,128)} %bitcast.8), calls=%async_computation.1 | async-start | bytes 65536 | tf_op jit(solution)/shard_map/all_to_all | solution.py:198
  39.7 0.7 add.83.refs_0_
  40.4 0.1 slice.73
  40.5 0.6 concatenate.19.refs_1_
  41.1 0.6 concatenate.21.refs_4_
  41.7 8.7 %all-to-all-done.1 = s32[64,1,64]{2,1,0:T(1,128)S(1)} async-done(((s32[64,1,64]{2,1,0:T(1,128)}), s32[64,1,64]{2,1,0:T(1,128)S(1)}, u32[]{:S(2)}, u32[]{:S(2)}) %all-to-all-start.1) | async-done | bytes 16416 | tf_op jit(solution)/shard_map/all_to_all | solution.py:198
  50.4 5.4 %all-to-all-start = ((bf16[4,128,128]{2,1,0:T(8,128)(2,1)}), bf16[4,128,128]{2,1,0:T(8,128)(2,1)S(1)}, u32[]{:S(2)}, u32[]{:S(2)}) async-start(bf16[4,128,128]{2,1,0:T(8,128)(2,1)} %bitcast), calls=%async_computation | async-start | bytes 262144 | tf_op jit(solution)/shard_map/all_to_all | solution.py:198
  55.9 2.3 fusion.27
  58.1 18.6 %encode.1 = bf16[4096,512]{1,0:T(8,128)(2,1)} custom-call(s32[1,4096]{1,0:T(1,128)} %add.83.refs_0_, bf16[8,4096]{1,0:T(8,128)(2,1)} %concatenate.19.refs_1_, bf16[512,512]{1,0:T(8,128)(2,1)} %refs_2_.1, bf16[512,512]{1,0:T(8,128)(2,1)} %get-tuple-element.15.refs_3_, bf16[8,512]{1,0:T(8,128)(2,1)} %concatenate.21.refs_4_, ...), custom_call_target="tpu_custom_call" | custom-call | tf_op jit(solution)/shard_map/encode/pallas_call | solution.py:78
  76.8 5.8 %all-to-all-start.2 = ((bf16[64,64,512]{2,1,0:T(8,128)(2,1)}), bf16[64,64,512]{2,1,0:T(8,128)(2,1)}, u32[]{:S(2)}, u32[]{:S(2)}) async-start(bf16[64,64,512]{2,1,0:T(8,128)(2,1)} %bitcast.45), calls=%async_computation.2 | async-start | bytes 8388608 | tf_op jit(solution)/shard_map/all_to_all | solution.py:198
  82.7 0.7 pad_maximum_fusion.2
  83.6 1.0 pad_maximum_fusion
  84.8 0.5 broadcast.121
  85.3 0.7 reduce.11
  86.1 0.7 reshape.144.ids
  86.8 0.7 copy_bitcast_fusion.1.base
  87.4 90.5 %all-to-all-done.2 = bf16[64,64,512]{2,1,0:T(8,128)(2,1)} async-done(((bf16[64,64,512]{2,1,0:T(8,128)(2,1)}), bf16[64,64,512]{2,1,0:T(8,128)(2,1)}, u32[]{:S(2)}, u32[]{:S(2)}) %all-to-all-start.2) | async-done | bytes 4194336 | tf_op jit(solution)/shard_map/all_to_all | solution.py:198
  177.9 7.5 %segment.1 = bf16[512,512]{1,0:T(8,128)(2,1)} custom-call(s32[1,4096]{1,0:T(1,128)} %reshape.144.ids, bf16[4096,512]{1,0:T(8,128)(2,1)} %bitcast.11.rows), custom_call_target="tpu_custom_call" | custom-call | tf_op jit(solution)/shard_map/segment/pallas_call | solution.py:112
  185.3 5.8 %all-to-all-start.3 = ((bf16[4,128,512]{2,1,0:T(8,128)(2,1)}), bf16[4,128,512]{2,1,0:T(8,128)(2,1)S(1)}, u32[]{:S(2)}, u32[]{:S(2)}) async-start(bf16[4,128,512]{2,1,0:T(8,128)(2,1)} %bitcast.46), calls=%async_computation.3 | async-start | bytes 1048576 | tf_op jit(solution)/shard_map/all_to_all | solution.py:198
  191.2 2.2 fusion.26
  193.4 3.0 %fusion.25 = (bf16[1024,512]{1,0:T(8,128)(2,1)}, bf16[1024,512]{1,0:T(8,128)(2,1)}) fusion(bf16[4096,512]{1,0:T(8,128)(2,1)} %all-gather.6.cloned.1.call-done), kind=kLoop, calls=%fused_computation.58 | loop fusion | bytes 4194304 | tf_op jit(solution)/shard_map/slice | solution.py:276
  196.4 2.6 all-to-all-done.3.parts
  199.0 0.8 copy-done.2
  199.8 3.0 %node.2.base = bf16[128,512]{1,0:T(8,128)(2,1)} custom-call(bf16[128,512]{1,0:T(8,128)(2,1)} %copy_bitcast_fusion.1.base, bf16[4,128,512]{2,1,0:T(8,128)(2,1)} %copy-done.2, bf16[1024,512]{1,0:T(8,128)(2,1)} %get-tuple-element.11.w_in, bf16[512,512]{1,0:T(8,128)(2,1)} %get-tuple-element.13.w_out, f32[2,512]{1,0:T(2,128)} %bias.3, f32[1,512]{1,0:T(1,128)} %bitcast.59), custom_call_target="tpu_custom_call" | custom-call | tf_op jit(solution)/shard_map/node/pallas_call | solution.py:138
  202.8 7.5 %all_gather.15.local = bf16[512,512]{1,0:T(8,128)(2,1)S(1)} all-gather(bf16[128,512]{1,0:T(8,128)(2,1)} %node.2.base), channel_id=1, replica_groups=mesh['lat'=64,'lon'=4] {'lon'}, dimensions={0}, use_global_device_ids=true | all-gather | bytes 655360 | tf_op jit(solution)/shard_map/all_gather | solution.py:261
  210.3 2.6 gather_fusion
  212.9 6.6 %all-to-all-start.4 = ((bf16[64,8,512]{2,1,0:T(8,128)(2,1)}), bf16[64,8,512]{2,1,0:T(8,128)(2,1)S(1)}, u32[]{:S(2)}, u32[]{:S(2)}) async-start(bf16[64,8,512]{2,1,0:T(8,128)(2,1)} %bitcast.16), calls=%async_computation.4 | async-start | bytes 1048576 | tf_op jit(solution)/shard_map/all_to_all | solution.py:198
  219.5 2.7 slice.94.w_in
  222.2 1.9 slice.95.w_out
  224.1 12.9 %all-to-all-done.4 = bf16[64,8,512]{2,1,0:T(8,128)(2,1)S(1)} async-done(((bf16[64,8,512]{2,1,0:T(8,128)(2,1)}), bf16[64,8,512]{2,1,0:T(8,128)(2,1)S(1)}, u32[]{:S(2)}, u32[]{:S(2)}) %all-to-all-start.4) | async-done | bytes 524320 | tf_op jit(solution)/shard_map/all_to_all | solution.py:198
  237.0 0.8 copy-done.1
  237.8 10.4 %edges.2 = (bf16[1024,512]{1,0:T(8,128)(2,1)}, bf16[512,512]{1,0:T(8,128)(2,1)}) custom-call(s32[1,1024]{1,0:T(1,128)} %bitcast.55, s32[1,1024]{1,0:T(1,128)} %bitcast.56, bf16[1024,512]{1,0:T(8,128)(2,1)} %edges.3, bf16[512,512]{1,0:T(8,128)(2,1)} %copy-done, bf16[512,512]{1,0:T(8,128)(2,1)} %bitcast.47, bf16[1536,512]{1,0:T(8,128)(2,1)} %slice.94.w_in, ...), custom_call_target="tpu_custom_call" | custom-call | tf_op jit(solution)/shard_map/edges/pallas_call | solution.py:170
  248.2 14.7 %all_to_all.35.parts = bf16[4,128,512]{2,1,0:T(8,128)(2,1)} all-to-all(bf16[4,128,512]{2,1,0:T(8,128)(2,1)} %bitcast.50), channel_id=1, replica_groups=mesh['lat'=64,'lon'=4] {'lon'}, dimensions={0} | all-to-all | bytes 1048576 | tf_op jit(solution)/shard_map/all_to_all | solution.py:198
  262.9 3.0 %node.3 = bf16[128,512]{1,0:T(8,128)(2,1)} custom-call(bf16[128,512]{1,0:T(8,128)(2,1)} %node.2.base, bf16[4,128,512]{2,1,0:T(8,128)(2,1)} %all_to_all.35.parts, bf16[1024,512]{1,0:T(8,128)(2,1)} %get-tuple-element.10.w_in, bf16[512,512]{1,0:T(8,128)(2,1)} %get-tuple-element.12.w_out, f32[2,512]{1,0:T(2,128)} %bias.5, f32[1,512]{1,0:T(1,128)} %bitcast.60), custom_call_target="tpu_custom_call" | custom-call | tf_op jit(solution)/shard_map/node/pallas_call | solution.py:138
  265.8 0.9 bitcast_bitcast_fusion
  266.8 7.0 %all_to_all.36 = bf16[4,128,128]{2,1,0:T(8,128)(2,1)S(1)} all-to-all(bf16[4,128,128]{2,1,0:T(8,128)(2,1)S(1)} %bitcast_bitcast_fusion), channel_id=1, replica_groups=mesh['lat'=64,'lon'=4] {'lon'}, dimensions={0} | all-to-all | bytes 262144 | tf_op jit(solution)/shard_map/all_to_all | solution.py:198
  273.7 0.7 copy.51
  (43 shorter events, 0.6 us)
Async XLA Ops:
  7.2 48.7 %all-gather.4.cloned.1.call-start = ((), (), s32[]{:S(2)}) async-start(), calls=%async_computation.7 | async-start | bytes 1310720 | tf_op jit(solution)/shard_map/all_gather | solution.py:230
  17.6 5.3 %copy-start.9 = (s32[2048,1]{0,1:T(1,128)S(1)}, s32[2048,1]{0,1:T(1,128)}, u32[]{:S(2)}) copy-start(s32[2048,1]{0,1:T(1,128)} %param.30) | copy-start | bytes 24580
  22.9 18.2 %copy-start.10 = (bf16[4,512]{1,0:T(4,128)(2,1)S(1)}, bf16[4,512]{1,0:T(4,128)(2,1)}, u32[]{:S(2)}) copy-start(bf16[4,512]{1,0:T(4,128)(2,1)} %param.38) | copy-start | bytes 12292
  24.6 25.9 %all-to-all-start.1 = ((s32[64,1,64]{2,1,0:T(1,128)}), s32[64,1,64]{2,1,0:T(1,128)S(1)}, u32[]{:S(2)}, u32[]{:S(2)}) async-start(s32[64,1,64]{2,1,0:T(1,128)} %bitcast.8), calls=%async_computation.1 | async-start | bytes 65536 | tf_op jit(solution)/shard_map/all_to_all | solution.py:198
  50.4 26.3 %all-to-all-start = ((bf16[4,128,128]{2,1,0:T(8,128)(2,1)}), bf16[4,128,128]{2,1,0:T(8,128)(2,1)S(1)}, u32[]{:S(2)}, u32[]{:S(2)}) async-start(bf16[4,128,128]{2,1,0:T(8,128)(2,1)} %bitcast), calls=%async_computation | async-start | bytes 262144 | tf_op jit(solution)/shard_map/all_to_all | solution.py:198
  76.8 5.9 %copy-start.7 = (bf16[128,512]{1,0:T(8,128)(2,1)S(1)}, bf16[128,512]{1,0:T(8,128)(2,1)}, u32[]{:S(2)}) copy-start(bf16[128,512]{1,0:T(8,128)(2,1)} %param.51) | copy-start | bytes 393220
  76.8 5.9 %copy-start.8 = (bf16[128,512]{1,0:T(8,128)(2,1)S(1)}, bf16[128,512]{1,0:T(8,128)(2,1)}, u32[]{:S(2)}) copy-start(bf16[128,512]{1,0:T(8,128)(2,1)} %param.43) | copy-start | bytes 393220
  76.8 6.7 %copy-start.3 = (bf16[1536,128]{1,0:T(8,128)(2,1)S(1)}, bf16[1536,128]{1,0:T(8,128)(2,1)}, u32[]{:S(2)}) copy-start(bf16[1536,128]{1,0:T(8,128)(2,1)} %param.46) | copy-start | bytes 1179652
  76.8 6.7 %copy-start.4 = (bf16[1024,128]{1,0:T(8,128)(2,1)S(1)}, bf16[1024,128]{1,0:T(8,128)(2,1)}, u32[]{:S(2)}) copy-start(bf16[1024,128]{1,0:T(8,128)(2,1)} %param.50) | copy-start | bytes 786436
  76.8 6.7 %copy-start.5 = (bf16[1024,128]{1,0:T(8,128)(2,1)S(1)}, bf16[1024,128]{1,0:T(8,128)(2,1)}, u32[]{:S(2)}) copy-start(bf16[1024,128]{1,0:T(8,128)(2,1)} %param.42) | copy-start | bytes 786436
  76.8 6.7 %copy-start.6 = (bf16[512,128]{1,0:T(8,128)(2,1)S(1)}, bf16[512,128]{1,0:T(8,128)(2,1)}, u32[]{:S(2)}) copy-start(bf16[512,128]{1,0:T(8,128)(2,1)} %param.47) | copy-start | bytes 393220
  76.8 101.0 %all-to-all-start.2 = ((bf16[64,64,512]{2,1,0:T(8,128)(2,1)}), bf16[64,64,512]{2,1,0:T(8,128)(2,1)}, u32[]{:S(2)}, u32[]{:S(2)}) async-start(bf16[64,64,512]{2,1,0:T(8,128)(2,1)} %bitcast.45), calls=%async_computation.2 | async-start | bytes 8388608 | tf_op jit(solution)/shard_map/all_to_all | solution.py:198
  82.6 2.0 copy-start.11
  82.7 108.5 %all-gather.8.cloned.1.call-start = ((), (), s32[]{:S(2)}) async-start(), calls=%async_computation.9 | async-start | bytes 1310720 | tf_op jit(solution)/shard_map/all_gather | solution.py:239
  83.5 109.9 %all-gather.6.cloned.1.call-start = ((), (), s32[]{:S(2)}) async-start(), calls=%async_computation.8 | async-start | bytes 5242880 | tf_op jit(solution)/shard_map/all_gather | solution.py:233
  185.3 13.7 %all-to-all-start.3 = ((bf16[4,128,512]{2,1,0:T(8,128)(2,1)}), bf16[4,128,512]{2,1,0:T(8,128)(2,1)S(1)}, u32[]{:S(2)}, u32[]{:S(2)}) async-start(bf16[4,128,512]{2,1,0:T(8,128)(2,1)} %bitcast.46), calls=%async_computation.3 | async-start | bytes 1048576 | tf_op jit(solution)/shard_map/all_to_all | solution.py:198
  199.0 0.8 copy-start.2
  210.3 2.6 copy-start
  212.9 24.1 %all-to-all-start.4 = ((bf16[64,8,512]{2,1,0:T(8,128)(2,1)}), bf16[64,8,512]{2,1,0:T(8,128)(2,1)S(1)}, u32[]{:S(2)}, u32[]{:S(2)}) async-start(bf16[64,8,512]{2,1,0:T(8,128)(2,1)} %bitcast.16), calls=%async_computation.4 | async-start | bytes 1048576 | tf_op jit(solution)/shard_map/all_to_all | solution.py:198
  237.0 0.8 copy-start.1
Sparse Core Ops, SparseCore 0:
  9.8 27.0 all-gather.3
  85.3 33.0 all-gather.7
  120.7 66.5 all-gather.5

commit v2 on v1

--- a/solution.py
+++ b/solution.py
@@ -13,6 +13,9 @@
 NODES = 512
 CAP = 64
 ROWS = NODES // LON
+PLANE = 32
+DEPTH = 8
+MESH = pl.DeviceIdType.MESH
 
 
 def matmul(a, b):
@@ -43,84 +46,350 @@
     return (lax.broadcasted_iota(jnp.int32, (count, width), 0) == row).astype(BF16)
 
 
-def slot_fields(owners, sender, node, feat):
-    count = owners.shape[0]
+def slots_kernel(owner, sender, node, feat, idx, fields):
+    count = owner.shape[1]
     block = 128
-    hit = (owners[:, None] == jnp.arange(LAT, dtype=jnp.int32)[None, :]).astype(BF16)
-    blocks = hit.reshape(count // block, block, LAT)
-    below = jnp.tril(jnp.ones((block, block), BF16), -1)
-    inside = jnp.einsum("ij,bjk->bik", below, blocks, preferred_element_type=F32)
-    totals = jnp.sum(blocks.astype(F32), axis=1)
-    earlier = jnp.tril(jnp.ones((count // block, count // block), F32), -1)
-    before = jnp.sum(earlier[:, :, None] * totals[None], axis=1)
-    rank = jnp.sum((inside + before[:, None, :]) * blocks.astype(F32), axis=2).reshape(count)
-    place = (rank.astype(jnp.int32)[:, None] == jnp.arange(CAP, dtype=jnp.int32)[None, :]).astype(BF16)
-    shifted = node + 1
-    values = [sender >> 8, sender & 255, shifted >> 8, shifted & 255]
-    values = [v.astype(BF16) for v in values] + [feat[i] for i in range(4)]
-    spread = jnp.concatenate([place * v[:, None] for v in values], axis=1)
-    slots = matmul_t(hit, spread).reshape(LAT, 8, CAP)
-    return jnp.moveaxis(slots, 1, 0).reshape(8, LAT * CAP)
-
-
-def encoder_kernel(step, sender, feat, grid, w_in, proj, w_out, bias, gain, out):
-    rows = matmul_t(one_hot(sender[...], WIDTH), grid[...]).astype(BF16)
-    pre = matmul(rows, w_in[...]) + (matmul_t(feat[...], proj[...]) + bias[0:1, :])
-    hidden = swish(pre).astype(BF16)
-    raw = matmul_nt(hidden, w_out[...])
-    out[...] = layer_norm(raw, gain[...], bias[1:2, :]).astype(BF16)
-
-
-def encode(sender, feat, grid, w_in, proj, w_out, bias, gain):
-    total = sender.shape[1]
-    step = 256
-    whole = lambda i: (0, 0)
+    owners = owner[...]
+    hit = one_hot(owners, LAT)
+    row = lax.broadcasted_iota(jnp.int32, (block, block), 0)
+    column = lax.broadcasted_iota(jnp.int32, (block, block), 1)
+    above = (row < column).astype(BF16)
+    carry = jnp.zeros((LAT, 1), F32)
+    ranks = []
+    for at in range(0, count, block):
+        part = hit[:, at : at + block]
+        wide = part.astype(F32)
+        before = matmul(part, above) + carry
+        ranks.append(jnp.sum(before * wide, axis=0, keepdims=True))
+        carry = carry + jnp.sum(wide, axis=1, keepdims=True)
+    rank = jnp.concatenate(ranks, axis=1).astype(jnp.int32)
+    half = owners // 32
+    target = (owners % 8) * 4 + (owners // 8) % 4
+    at_target = one_hot(target, PLANE)
+    place = one_hot(rank + half * CAP, 2 * CAP).astype(F32)
+    named = node[...] + half * NODES + 1
+
+    def put(values):
+        return matmul_nt(at_target, (place * values.astype(F32)).astype(BF16))
+
+    def put_whole(values):
+        return (put(values // 32) * 32.0 + put(values % 32)).astype(jnp.int32)
+
+    idx[:, :128] = put_whole(sender[...])
+    idx[:, 128:] = put_whole(named) - 1
+    for i in range(4):
+        fields[:, i * 128 : (i + 1) * 128] = put(feat[i : i + 1, :])
+    fields[:, 512:] = jnp.zeros((PLANE, 512), F32)
+
+
+def slots(owner, sender, node, feat):
     return pl.pallas_call(
-        lambda *refs: encoder_kernel(step, *refs),
-        grid=(total // step,),
-        in_specs=[
-            pl.BlockSpec((1, step), lambda i: (0, i)),
-            pl.BlockSpec((8, step), lambda i: (0, i)),
-            pl.BlockSpec((512, WIDTH), whole),
-            pl.BlockSpec((WIDTH, WIDTH), whole),
-            pl.BlockSpec((8, WIDTH), whole),
-            pl.BlockSpec((WIDTH, WIDTH), whole),
-            pl.BlockSpec((2, WIDTH), whole),
-            pl.BlockSpec((1, WIDTH), whole),
+        slots_kernel,
+        out_shape=[
+            jax.ShapeDtypeStruct((PLANE, 256), jnp.int32),
+            jax.ShapeDtypeStruct((PLANE, 1024), F32),
         ],
-        out_specs=pl.BlockSpec((step, WIDTH), lambda i: (i, 0)),
-        out_shape=jax.ShapeDtypeStruct((total, WIDTH), BF16),
-        name="encode",
-    )(sender, feat, grid, w_in, proj, w_out, bias, gain)
-
-
-def segment_kernel(ids, rows, out, acc):
-    @pl.when(pl.program_id(0) == 0)
-    def _():
-        acc[...] = jnp.zeros_like(acc)
-
-    acc[...] += matmul(one_hot(ids[...], NODES), rows[...])
-
-    @pl.when(pl.program_id(0) == pl.num_programs(0) - 1)
-    def _():
-        out[...] = acc[...].astype(BF16)
-
-
-def segment_sum(ids, rows):
-    total = rows.shape[0]
-    step = 512
+        name="slots",
+    )(owner, sender, node, feat)
+
+
+def remote(source, target, send, receive, where):
+    return pltpu.make_async_remote_copy(
+        src_ref=source,
+        dst_ref=target,
+        send_sem=send,
+        recv_sem=receive,
+        device_id=where,
+        device_id_type=MESH,
+    )
+
+
+def gather_kernel(
+    idx, feat, grid, w_in, proj, w_out, bias, gain, mesh, node_in, node_out, node_bias, node_gain,
+    out,
+    send, got, got_ids, acc, part, plane, share, aggregate, base, middle, whole,
+    s_msg, r_msg, s_ids, r_ids, s_z, r_z, s_share, r_share, s_base, r_base, s_mid, r_mid,
+):
+    lat = lax.axis_index("lat")
+    lon = lax.axis_index("lon")
+    z = lat // 8
+    cell = lat % 8
+    place = cell * LON + lon
+    owner = z % 4 == lon
+
+    def at_place(t):
+        return {"lat": z * 8 + t // LON, "lon": t % LON}
+
+    def at_depth(depth):
+        return {"lat": depth * 8 + cell, "lon": lon}
+
+    def beside(step):
+        return {"lat": lat, "lon": (lon + step) % LON}
+
+    barrier = pltpu.get_barrier_semaphore()
+
+    def greet(d, _):
+        pl.semaphore_signal(barrier, inc=1, device_id=at_place((place + d) % PLANE), device_id_type=MESH)
+        return 0
+
+    lax.fori_loop(1, PLANE, greet, 0)
+
+    @pl.when(owner)
+    def _():
+        def greet_all(d, _):
+            pl.semaphore_signal(barrier, inc=1, device_id=at_depth((z + d) % DEPTH), device_id_type=MESH)
+            return 0
+
+        lax.fori_loop(1, DEPTH, greet_all, 0)
+
+    @pl.when(z % 4 != lon)
+    def _():
+        pl.semaphore_signal(barrier, inc=1, device_id=at_depth(lon), device_id_type=MESH)
+        pl.semaphore_signal(barrier, inc=1, device_id=at_depth(lon + 4), device_id_type=MESH)
+
+    def target(d):
+        return (place + d) % PLANE
+
+    def compute(d):
+        one, two = target(d), target(d + 1)
+        sender = jnp.concatenate([idx[one][0:1, :], idx[two][0:1, :]], axis=1)
+        features = jnp.concatenate([feat[one], feat[two]], axis=1).astype(BF16)
+        rows = matmul_t(one_hot(sender, WIDTH), grid[...]).astype(BF16)
+        pre = matmul(rows, w_in[...]) + (matmul_t(features, proj[...]) + bias[0:1, :])
+        raw = matmul_nt(swish(pre).astype(BF16), w_out[...])
+        message = layer_norm(raw, gain[...], bias[1:2, :]).astype(BF16)
+        send[d] = message[:128]
+        send[d + 1] = message[128:]
+
+    def message_copy(d):
+        return remote(send.at[d], got.at[d], s_msg.at[d], r_msg.at[d], at_place(target(d)))
+
+    def ids_copy(d):
+        return remote(idx.at[target(d)], got_ids.at[d], s_ids.at[d], r_ids.at[d], at_place(target(d)))
+
+    def base_copy(step):
+        other = (lon + step) % LON
+        return remote(
+            mesh.at[pl.ds(pl.multiple_of(other * ROWS, ROWS), ROWS), :],
+            base.at[:, pl.ds(pl.multiple_of(lon * ROWS, ROWS), ROWS)],
+            s_base.at[step],
+            r_base.at[step],
+            beside(step),
+        )
+
+    def base_arrival(step):
+        other = (lon - step + LON) % LON
+        return remote(
+            mesh.at[pl.ds(0, ROWS), :],
+            base.at[:, pl.ds(pl.multiple_of(other * ROWS, ROWS), ROWS)],
+            s_base.at[step],
+            r_base.at[step],
+            beside(step),
+        )
+
+    compute(0)
+    got[0] = send[0]
+    got_ids[0] = idx[place]
+
+    @pl.when(owner)
+    def _():
+        pl.semaphore_wait(barrier, PLANE - 1 + DEPTH - 1)
+
+    @pl.when(z % 4 != lon)
+    def _():
+        pl.semaphore_wait(barrier, PLANE - 1 + 2)
+
+    message_copy(1).start()
+
+    def start_ids(d, _):
+        ids_copy(d).start()
+        return 0
+
+    lax.fori_loop(1, PLANE, start_ids, 0)
+
+    def start_messages(s, _):
+        compute(2 * s)
+        message_copy(2 * s).start()
+        message_copy(2 * s + 1).start()
+        return 0
+
+    lax.fori_loop(1, PLANE // 2, start_messages, 0)
+    for step in range(1, LON):
+        base_copy(step).start()
+    mine = pl.ds(pl.multiple_of(lon * ROWS, ROWS), ROWS)
+    base[:, mine] = mesh[mine, :]
+
+    acc[...] = jnp.zeros_like(acc)
+
+    def take(g):
+        ids = jnp.concatenate([got_ids[4 * g + i][1:2, :] for i in range(4)], axis=1)
+        rows = jnp.concatenate([got[4 * g + i] for i in range(4)], axis=0)
+        acc[...] += matmul(one_hot(ids, 2 * NODES), rows)
+
+    def arrive(d):
+        ids_copy(d).wait_recv()
+        message_copy(d).wait_recv()
+
+    for d in range(1, 4):
+        arrive(d)
+    take(0)
+
+    def collect(g, _):
+        for i in range(4):
+            arrive(4 * g + i)
+        take(g)
+        return 0
+
+    lax.fori_loop(1, PLANE // 4, collect, 0)
+
+    def depth_copy(j, q):
+        depth = lon + 4 * j
+        away = (depth - z + DEPTH) % DEPTH
+        return remote(
+            part.at[pl.ds(j * NODES + q * ROWS, ROWS), :],
+            plane.at[away, pl.ds(q * ROWS, ROWS), :],
+            s_z.at[j, q],
+            r_z.at[away, q],
+            at_depth(depth),
+        )
+
+    for q in range(LON):
+        for j in range(2):
+            rows = pl.ds(j * NODES + q * ROWS, ROWS)
+            part[rows, :] = acc[rows, :].astype(BF16)
+
+            @pl.when(z != lon + 4 * j)
+            def _():
+                depth_copy(j, q).start()
+
+    def share_copy(q):
+        return remote(share.at[q], aggregate, s_share.at[q], r_share.at[0], {"lat": lat, "lon": q})
+
+    @pl.when(owner)
+    def _():
+        for q in range(LON):
+            first = pl.multiple_of((z // 4) * NODES + q * ROWS, ROWS)
+            total = acc[pl.ds(first, ROWS), :]
+            for away in range(1, DEPTH):
+                remote(
+                    part.at[pl.ds(0, ROWS), :],
+                    plane.at[away, pl.ds(q * ROWS, ROWS), :],
+                    s_z.at[0, q],
+                    r_z.at[away, q],
+                    at_depth(z),
+                ).wait_recv()
+                total = total + plane[away, pl.ds(q * ROWS, ROWS), :].astype(F32)
+            rounded = total.astype(BF16)
+
+            @pl.when(lon == q)
+            def _():
+                aggregate[...] = rounded
+
+            @pl.when(lon != q)
+            def _():
+                share[q] = rounded
+                share_copy(q).start()
+
+    for step in range(1, LON):
+        base_arrival(step).wait_recv()
+    before = base[...]
+    pre_base = matmul(before, node_in[:WIDTH, :])
+
+    @pl.when(z % 4 != lon)
+    def _():
+        share_copy(0).wait_recv()
+
+    pre = pre_base + matmul(aggregate[...], node_in[WIDTH:, :]) + node_bias[0:1, :]
+    raw = matmul(swish(pre).astype(BF16), node_out[...])
+    updated = before.astype(F32) + layer_norm(raw, node_gain[...], node_bias[1:2, :])
+    middle[...] = updated.astype(BF16)
+
+    def middle_copy(step):
+        return remote(
+            middle,
+            whole.at[pl.ds(pl.multiple_of(lon * ROWS, ROWS), ROWS), :],
+            s_mid.at[step],
+            r_mid.at[step],
+            beside(step),
+        )
+
+    def middle_arrival(step):
+        other = (lon - step + LON) % LON
+        return remote(
+            middle,
+            whole.at[pl.ds(pl.multiple_of(other * ROWS, ROWS), ROWS), :],
+            s_mid.at[step],
+            r_mid.at[step],
+            beside(step),
+        )
+
+    for step in range(1, LON):
+        middle_copy(step).start()
+    whole[mine, :] = middle[...]
+    for step in range(1, LON):
+        middle_arrival(step).wait_recv()
+    out[...] = whole[...]
+
+    def sent(d, _):
+        ids_copy(d).wait_send()
+        message_copy(d).wait_send()
+        return 0
+
+    lax.fori_loop(1, PLANE, sent, 0)
+    for step in range(1, LON):
+        base_copy(step).wait_send()
+        middle_copy(step).wait_send()
+    for q in range(LON):
+        for j in range(2):
+
+            @pl.when(z != lon + 4 * j)
+            def _():
+                depth_copy(j, q).wait_send()
+
+    @pl.when(owner)
+    def _():
+        for q in range(LON):
+
+            @pl.when(lon != q)
+            def _():
+                share_copy(q).wait_send()
+
+
+def gather_nodes(*operands):
+    dma = pltpu.SemaphoreType.DMA
     return pl.pallas_call(
-        segment_kernel,
-        grid=(total // step,),
-        in_specs=[
-            pl.BlockSpec((1, step), lambda i: (0, i)),
-            pl.BlockSpec((step, WIDTH), lambda i: (i, 0)),
+        gather_kernel,
+        in_specs=[pl.BlockSpec(memory_space=pltpu.VMEM)] * len(operands),
+        out_specs=pl.BlockSpec(memory_space=pltpu.VMEM),
+        out_shape=jax.ShapeDtypeStruct((NODES, WIDTH), BF16),
+        scratch_shapes=[
+            pltpu.VMEM((PLANE, 128, WIDTH), BF16),
+            pltpu.VMEM((PLANE, 128, WIDTH), BF16),
+            pltpu.VMEM((PLANE, 2, 128), jnp.int32),
+            pltpu.VMEM((2 * NODES, WIDTH), F32),
+            pltpu.VMEM((2 * NODES, WIDTH), BF16),
+            pltpu.VMEM((DEPTH, NODES, WIDTH), BF16),
+            pltpu.VMEM((LON, ROWS, WIDTH), BF16),
+            pltpu.VMEM((ROWS, WIDTH), BF16),
+            pltpu.VMEM((ROWS, WIDTH), BF16),
+            pltpu.VMEM((ROWS, WIDTH), BF16),
+            pltpu.VMEM((NODES, WIDTH), BF16),
+            dma((PLANE,)),
+            dma((PLANE,)),
+            dma((PLANE,)),
+            dma((PLANE,)),
+            dma((2, LON)),
+            dma((DEPTH, LON)),
+            dma((LON,)),
+            dma((1,)),
+            dma((LON,)),
+            dma((LON,)),
+            dma((LON,)),
+            dma((LON,)),
         ],
-        out_specs=pl.BlockSpec((NODES, WIDTH), lambda i: (0, 0)),
-        out_shape=jax.ShapeDtypeStruct((NODES, WIDTH), BF16),
-        scratch_shapes=[pltpu.VMEM((NODES, WIDTH), F32)],
-        name="segment",
-    )(ids, rows)
+        compiler_params=pltpu.CompilerParams(collective_id=0, has_side_effects=True),
+        name="gather_nodes",
+    )(*operands)
 
 
 def node_kernel(base, parts, w_in, w_out, bias, gain, out):
@@ -239,26 +508,26 @@
     outer = lax.all_gather(
         jnp.concatenate([enc_node_out, proc_node_out], 1), "lon", axis=0, tiled=True
     )
-    base = swap(mesh_latent.reshape(LON, ROWS, ROWS), "lon")
-    base = jnp.moveaxis(base, 0, 1).reshape(ROWS, WIDTH)
-
-    fields = slot_fields(grid_owner[:, 0], grid_sender, grid_node, grid_feat)
-    whole = fields[:4].astype(jnp.int32)
-    sender = (whole[0] * 256 + whole[1]).reshape(1, -1)
-    node = (whole[2] * 256 + whole[3] - 1).reshape(LAT, 1, CAP)
-    feat = jnp.concatenate([fields[4:], jnp.zeros((4, LAT * CAP), F32)], 0).astype(BF16)
+    idx, fields = slots(
+        grid_owner.reshape(1, -1), grid_sender.reshape(1, -1), grid_node.reshape(1, -1), grid_feat
+    )
     proj = jnp.concatenate([enc_feat_proj, jnp.zeros((4, WIDTH), BF16)], 0)
-    ids = swap(node, "lat")
-    messages = encode(
-        sender, feat, grid_latent, first[:WIDTH], proj, first[WIDTH:], enc_edge_bias, enc_edge_gain[None]
-    )
-    arrived = swap(messages.reshape(LAT, CAP, WIDTH), "lat").reshape(LAT * CAP, WIDTH)
-    partial = segment_sum(ids.reshape(1, LAT * CAP), arrived)
-    parts = swap(partial.reshape(LON, ROWS, WIDTH), "lon")
-    middle = node_network(
-        base, parts, inner[:1024], outer[:, :WIDTH], enc_node_bias, enc_node_gain[None]
-    )
-    mesh_mid = lax.all_gather(middle, "lon", axis=0, tiled=True)
+    mesh_mid = gather_nodes(
+        idx.reshape(PLANE, 2, 128),
+        fields.reshape(PLANE, 8, 128),
+        grid_latent,
+        first[:WIDTH],
+        proj,
+        first[WIDTH:],
+        enc_edge_bias,
+        enc_edge_gain[None],
+        mesh_latent,
+        inner[:1024],
+        outer[:, :WIDTH],
+        enc_node_bias,
+        enc_node_gain[None],
+    )
+    middle = lax.dynamic_slice_in_dim(mesh_mid, lax.axis_index("lon") * ROWS, ROWS, 0)
     halo = swap(mesh_mid[halo_send], "lat").reshape(NODES, WIDTH)
     edge_update, partial = edge_network(
         mesh_sender.reshape(1, -1),

time: 282 us -> 316 us (1.12)
  Pallas kernels: 42.4 us -> 142 us
  starting transfers between devices: 38.8 us -> 11.7 us
  blocking collectives: 29.2 us -> 7.08 us
  other arithmetic: 11.4 us -> 5.62 us
  waiting for transfers between devices: 115 us -> 110 us
  local copies, waits for them, and re-layouts: 28.5 us -> 24.3 us
    pallas_call x2, Pallas kernels: 26.1 us -> 129 us  [the longest x1 126 us: gather_nodes(): pl.pallas_call(gather_kernel, in_specs=[pl.BlockSpec(memory_space=pltpu.V...]
    all_to_all x5 -> x2, waiting for transfers between devices: 115 us -> 19 us  [swap(): return lax.all_to_all(tiles, axis, split_axis=0, concat_axis=0, tiled=True)]
    all_gather x1, waiting for transfers between devices: 0.01 us -> 50.7 us  [local(): lax.all_gather(jnp.concatenate([enc_node_in, proc_edge_in, proc_edge_out,...]
    all_to_all x5 -> x2, starting transfers between devices: 38.7 us -> 11.6 us  [swap(): return lax.all_to_all(tiles, axis, split_axis=0, concat_axis=0, tiled=True)]
    all_gather x1, waiting for transfers between devices: 0.01 us -> 23.3 us  [local(): lax.all_gather(jnp.concatenate([enc_edge_in, enc_edge_out], 0), 'lon', ax...]
    all_gather x1, waiting for transfers between devices: 0.01 us -> 17.2 us  [local(): lax.all_gather(jnp.concatenate([enc_node_out, proc_node_out], 1), 'lon',...]
    all_to_all x2 -> x1, blocking collectives: 21.7 us -> 7.08 us  [swap(): return lax.all_to_all(tiles, axis, split_axis=0, concat_axis=0, tiled=True)]
    all_gather x1 -> x0, blocking collectives: 7.51 us -> none  [local(): mesh_mid = lax.all_gather(middle, 'lon', axis=0, tiled=True)]
  transfers between devices with their start and end apart: 8 -> 5, of which waited for: 4 -> 5; matrix products, arithmetic and copies ran while one was open for 12% -> 6% of each run, Pallas kernels for 9% -> 1%
where the time goes in v2:
time: 316 us; the launch traced here: 315 us
  Pallas kernels  142 us (45%)
  waiting for transfers between devices  110 us (35%)
  local copies, waits for them, and re-layouts  24.3 us (8%)
  between operations  13.8 us (4%)
  starting transfers between devices  11.7 us (4%)
  blocking collectives  7.08 us (2%)
  other arithmetic  5.62 us (2%)
    pallas_call x1, Pallas kernels, gather_nodes(): pl.pallas_call(gather_kernel, in_specs=[pl.BlockSpec(memory_space=pltpu.V...  126 us
    all_gather x1, waiting for transfers between devices, local(): lax.all_gather(jnp.concatenate([enc_node_in, proc_edge_in, proc_edge_out,...  50.7 us
    all_gather x1, waiting for transfers between devices, local(): lax.all_gather(jnp.concatenate([enc_edge_in, enc_edge_out], 0), 'lon', ax...  23.3 us
    all_to_all x2, waiting for transfers between devices, swap(): return lax.all_to_all(tiles, axis, split_axis=0, concat_axis=0, tiled=True)  19 us
    all_gather x1, waiting for transfers between devices, local(): lax.all_gather(jnp.concatenate([enc_node_out, proc_node_out], 1), 'lon',...  17.2 us
    all_to_all x2, starting transfers between devices, swap(): return lax.all_to_all(tiles, axis, split_axis=0, concat_axis=0, tiled=True)  11.6 us
    pallas_call x1, Pallas kernels, edge_network(): pl.pallas_call(edge_kernel, grid=(total // step,), in_specs=[pl.BlockSpec...  10.4 us
    all_to_all x1, blocking collectives, swap(): return lax.all_to_all(tiles, axis, split_axis=0, concat_axis=0, tiled=True)  7.08 us
  transfers between devices with their start and end apart: 5, of which 5 were waited for; matrix products, arithmetic and copies ran while one was open for 6% of the time, Pallas kernels for 1%

profile of v2, /device:TPU:1, one launch (start us, length us, event | category | flops | bytes accessed | tf_op | source)
XLA Modules:
  0.0 315.2 jit_solution(3538557668030434039)
XLA Ops:
  7.2 0.0 all-gather.8.cloned.1.call-start
  7.2 1.7 pad_maximum_fusion.2
  8.9 0.0 all-gather.8.cloned.1.call-update
  8.9 0.0 copy-start.3
  8.9 0.0 copy-start.2
  8.9 0.0 all-gather.4.cloned.1.call-start
  9.0 1.7 pad_maximum_fusion.1
  10.7 0.0 all-gather.4.cloned.1.call-update
  10.7 0.0 all-gather.6.cloned.1.call-start
  10.7 2.3 pad_maximum_fusion
  13.0 0.0 all-gather.6.cloned.1.call-update
  13.0 3.2 %slots.1 = (s32[32,256]{1,0:T(8,128)}, f32[32,1024]{1,0:T(8,128)}) custom-call(s32[1,2048]{1,0:T(1,128)} %bitcast.27, s32[1,2048]{1,0:T(1,128)} %bitcast.28, s32[1,2048]{1,0:T(1,128)} %bitcast.29, bf16[4,2048]{1,0:T(4,128)(2,1)} %feat.1), custom_call_target="tpu_custom_call" | custom-call | tf_op jit(solution)/shard_map/slots/pallas_call | solution.py:86
  16.2 1.6 copy.35
  17.8 1.4 reshape.40.idx
  19.2 0.0 copy-done.3
  19.2 0.1 copy.32
  19.3 0.1 reshape.50
  19.4 0.0 copy-done.2
  19.4 0.6 concatenate.13.proj
  20.0 17.2 %all-gather.8.cloned.1.call-done = bf16[512,1024]{1,0:T(8,128)(2,1)} async-done(((bf16[128,1024]{1,0:T(8,128)(2,1)}), bf16[512,1024]{1,0:T(8,128)(2,1)}) %all-gather.8.cloned.1.call-update) | async-done | bytes 1048592 | tf_op jit(solution)/shard_map/all_gather | solution.py:508
  37.2 2.3 fusion.1
  39.5 23.3 %all-gather.4.cloned.1.call-done = bf16[1024,512]{1,0:T(8,128)(2,1)} async-done(((bf16[1024,128]{1,0:T(8,128)(2,1)}), bf16[1024,512]{1,0:T(8,128)(2,1)}) %all-gather.4.cloned.1.call-update) | async-done | bytes 1048592 | tf_op jit(solution)/shard_map/all_gather | solution.py:499
  62.8 2.2 fusion.2
  65.1 50.7 %all-gather.6.cloned.1.call-done = bf16[4096,512]{1,0:T(8,128)(2,1)} async-done(((bf16[4096,128]{1,0:T(8,128)(2,1)}), bf16[4096,512]{1,0:T(8,128)(2,1)}) %all-gather.6.cloned.1.call-update) | async-done | bytes 4194320 | tf_op jit(solution)/shard_map/all_gather | solution.py:502
  115.8 3.0 fusion
  118.8 125.8 %gather_nodes.1.local = bf16[512,512]{1,0:T(8,128)(2,1)} custom-call(s32[32,2,128]{2,1,0:T(2,128)} %reshape.40.idx, f32[32,8,128]{2,1,0:T(8,128)} %bitcast.23, bf16[512,512]{1,0:T(8,128)(2,1)} %grid.1, bf16[512,512]{1,0:T(8,128)(2,1)} %get-tuple-element.15.w_in, bf16[8,512]{1,0:T(8,128)(2,1)} %concatenate.13.proj, bf16[512,512]{1,0:T(8,128)(2,1)} %get-tuple-element.14.w_out, ...), custom_call_target="tpu_custom_call" | custom-call | tf_op jit(solution)/shard_map/gather_nodes/pallas_call | solution.py:360
  244.5 3.8 %gather_fusion = bf16[512,512]{1,0:T(8,128)(2,1)} fusion(bf16[512,512]{1,0:T(8,128)(2,1)} %gather_nodes.1.local, s32[1024]{0:T(1024)S(1)} %pad_clamp_fusion), kind=kCustom, calls=%fused_computation | custom fusion | bytes 1050624 | tf_op jit(solution)/shard_map/gather | solution.py:531
  248.3 8.2 %all-to-all-start = ((bf16[64,8,512]{2,1,0:T(8,128)(2,1)}), bf16[64,8,512]{2,1,0:T(8,128)(2,1)S(1)}, u32[]{:S(2)}, u32[]{:S(2)}) async-start(bf16[64,8,512]{2,1,0:T(8,128)(2,1)} %bitcast.7), calls=%async_computation | async-start | bytes 1048576 | tf_op jit(solution)/shard_map/all_to_all | solution.py:467
  256.5 2.7 slice.38.w_in
  259.1 1.9 slice.39.w_out
  261.0 14.2 %all-to-all-done = bf16[64,8,512]{2,1,0:T(8,128)(2,1)S(1)} async-done(((bf16[64,8,512]{2,1,0:T(8,128)(2,1)}), bf16[64,8,512]{2,1,0:T(8,128)(2,1)S(1)}, u32[]{:S(2)}, u32[]{:S(2)}) %all-to-all-start) | async-done | bytes 524320 | tf_op jit(solution)/shard_map/all_to_all | solution.py:467
  275.2 0.0 copy-start
  275.2 0.8 copy-done
  276.0 10.4 %edges.2 = (bf16[1024,512]{1,0:T(8,128)(2,1)}, bf16[512,512]{1,0:T(8,128)(2,1)}) custom-call(s32[1,1024]{1,0:T(1,128)} %bitcast.30, s32[1,1024]{1,0:T(1,128)} %bitcast.31, bf16[1024,512]{1,0:T(8,128)(2,1)} %edges.3, bf16[512,512]{1,0:T(8,128)(2,1)} %gather_nodes.1.local, bf16[512,512]{1,0:T(8,128)(2,1)} %bitcast.22, bf16[1536,512]{1,0:T(8,128)(2,1)} %slice.38.w_in, ...), custom_call_target="tpu_custom_call" | custom-call | tf_op jit(solution)/shard_map/edges/pallas_call | solution.py:439
  286.4 3.5 %all-to-all-start.1 = ((bf16[4,128,512]{2,1,0:T(8,128)(2,1)}), bf16[4,128,512]{2,1,0:T(8,128)(2,1)S(1)}, u32[]{:S(2)}, u32[]{:S(2)}) async-start(bf16[4,128,512]{2,1,0:T(8,128)(2,1)} %bitcast.24), calls=%async_computation.1 | async-start | bytes 1048576 | tf_op jit(solution)/shard_map/all_to_all | solution.py:467
  289.9 1.6 constant_dynamic-slice_fusion.base
  291.5 4.8 %all-to-all-done.1.parts = bf16[4,128,512]{2,1,0:T(8,128)(2,1)S(1)} async-done(((bf16[4,128,512]{2,1,0:T(8,128)(2,1)}), bf16[4,128,512]{2,1,0:T(8,128)(2,1)S(1)}, u32[]{:S(2)}, u32[]{:S(2)}) %all-to-all-start.1) | async-done | bytes 524320 | tf_op jit(solution)/shard_map/all_to_all | solution.py:467
  296.3 0.0 copy-start.1
  296.3 0.8 copy-done.1
  297.1 3.0 node.1
  300.0 0.9 bitcast_bitcast_fusion
  301.0 7.1 %all_to_all.15 = bf16[4,128,128]{2,1,0:T(8,128)(2,1)S(1)} all-to-all(bf16[4,128,128]{2,1,0:T(8,128)(2,1)S(1)} %bitcast_bitcast_fusion), channel_id=1, replica_groups=mesh['lat'=64,'lon'=4] {'lon'}, dimensions={0} | all-to-all | bytes 262144 | tf_op jit(solution)/shard_map/all_to_all | solution.py:467
  308.0 0.7 copy.38
  (2 shorter events, 0.0 us)
Async XLA Ops:
  7.2 30.0 %all-gather.8.cloned.1.call-start = ((), (), s32[]{:S(2)}) async-start(), calls=%async_computation.5 | async-start | bytes 1310720 | tf_op jit(solution)/shard_map/all_gather | solution.py:508
  8.9 10.3 %copy-start.3 = (s32[64,8]{0,1:T(8,128)S(1)}, s32[64,8]{0,1:T(8,128)}, u32[]{:S(2)}) copy-start(s32[64,8]{0,1:T(8,128)} %param.34) | copy-start | bytes 6148
  8.9 10.4 %copy-start.2 = (bf16[4,512]{1,0:T(4,128)(2,1)S(1)}, bf16[4,512]{1,0:T(4,128)(2,1)}, u32[]{:S(2)}) copy-start(bf16[4,512]{1,0:T(4,128)(2,1)} %param.38) | copy-start | bytes 12292
  8.9 53.9 %all-gather.4.cloned.1.call-start = ((), (), s32[]{:S(2)}) async-start(), calls=%async_computation.3 | async-start | bytes 1310720 | tf_op jit(solution)/shard_map/all_gather | solution.py:499
  10.7 105.1 %all-gather.6.cloned.1.call-start = ((), (), s32[]{:S(2)}) async-start(), calls=%async_computation.4 | async-start | bytes 5242880 | tf_op jit(solution)/shard_map/all_gather | solution.py:502
  248.3 27.0 %all-to-all-start = ((bf16[64,8,512]{2,1,0:T(8,128)(2,1)}), bf16[64,8,512]{2,1,0:T(8,128)(2,1)S(1)}, u32[]{:S(2)}, u32[]{:S(2)}) async-start(bf16[64,8,512]{2,1,0:T(8,128)(2,1)} %bitcast.7), calls=%async_computation | async-start | bytes 1048576 | tf_op jit(solution)/shard_map/all_to_all | solution.py:467
  275.2 0.8 copy-start
  286.4 9.8 %all-to-all-start.1 = ((bf16[4,128,512]{2,1,0:T(8,128)(2,1)}), bf16[4,128,512]{2,1,0:T(8,128)(2,1)S(1)}, u32[]{:S(2)}, u32[]{:S(2)}) async-start(bf16[4,128,512]{2,1,0:T(8,128)(2,1)} %bitcast.24), calls=%async_computation.1 | async-start | bytes 1048576 | tf_op jit(solution)/shard_map/all_to_all | solution.py:467
  296.3 0.8 copy-start.1
Sparse Core Ops, SparseCore 0:
  9.8 27.3 all-gather.7
  39.0 23.7 all-gather.3
  65.2 50.5 all-gather.5

commit v3 on v2

v3 whole, which is shorter than its diff:
```python
import jax
import jax.numpy as jnp
from jax import lax
from jax.experimental import pallas as pl
from jax.experimental.pallas import tpu as pltpu
from jax.sharding import PartitionSpec as P

F32 = jnp.float32
BF16 = jnp.bfloat16
LAT = 64
LON = 4
WIDTH = 512
NODES = 512
CAP = 64
ROWS = NODES // LON
PLANE = 32
DEPTH = 8
MESH = pl.DeviceIdType.MESH


def matmul(a, b):
    return jnp.dot(a, b, preferred_element_type=F32)


def matmul_t(a, b):
    return lax.dot_general(a, b, (((0,), (0,)), ((), ())), preferred_element_type=F32)


def matmul_nt(a, b):
    return lax.dot_general(a, b, (((1,), (1,)), ((), ())), preferred_element_type=F32)


def swish(t):
    return t / (1.0 + jnp.exp(-t))


def layer_norm(values, gain, offset):
    average = jnp.mean(values, axis=-1, keepdims=True)
    centred = values - average
    spread = jnp.mean(centred * centred, axis=-1, keepdims=True)
    return centred * lax.rsqrt(spread + 1e-05) * gain + offset


def one_hot(row, count):
    width = row.shape[1]
    return (lax.broadcasted_iota(jnp.int32, (count, width), 0) == row).astype(BF16)


def slots_kernel(owner, sender, node, feat, idx, fields):
    count = owner.shape[1]
    block = 128
    owners = owner[...]
    hit = one_hot(owners, LAT)
    row = lax.broadcasted_iota(jnp.int32, (block, block), 0)
    column = lax.broadcasted_iota(jnp.int32, (block, block), 1)
    above = (row < column).astype(BF16)
    carry = jnp.zeros((LAT, 1), F32)
    ranks = []
    for at in range(0, count, block):
        part = hit[:, at : at + block]
        wide = part.astype(F32)
        before = matmul(part, above) + carry
        ranks.append(jnp.sum(before * wide, axis=0, keepdims=True))
        carry = carry + jnp.sum(wide, axis=1, keepdims=True)
    rank = jnp.concatenate(ranks, axis=1).astype(jnp.int32)
    half = owners // 32
    target = (owners % 8) * 4 + (owners // 8) % 4
    at_target = one_hot(target, PLANE)
    place = one_hot(rank + half * CAP, 2 * CAP).astype(F32)
    named = node[...] + half * NODES + 1

    def put(values):
        return matmul_nt(at_target, (place * values.astype(F32)).astype(BF16))

    def put_whole(values):
        return (put(values // 32) * 32.0 + put(values % 32)).astype(jnp.int32)

    idx[:, :128] = put_whole(sender[...])
    idx[:, 128:] = put_whole(named) - 1
    for i in range(4):
        fields[:, i * 128 : (i + 1) * 128] = put(feat[i : i + 1, :])
    fields[:, 512:] = jnp.zeros((PLANE, 512), F32)


def slots(owner, sender, node, feat):
    return pl.pallas_call(
        slots_kernel,
        out_shape=[
            jax.ShapeDtypeStruct((PLANE, 256), jnp.int32),
            jax.ShapeDtypeStruct((PLANE, 1024), F32),
        ],
        name="slots",
    )(owner, sender, node, feat)


def remote(source, target, send, receive, where):
    return pltpu.make_async_remote_copy(
        src_ref=source,
        dst_ref=target,
        send_sem=send,
        recv_sem=receive,
        device_id=where,
        device_id_type=MESH,
    )


COLUMNS = (True, True, True, False, True, True, True, False)


def layer_kernel(
    idx, feat, grid, mesh, halo_rows, edges, sender, receiver, proj,
    edge_bias, edge_gain, node_bias, node_gain, proc_bias, proc_gain, last_bias, last_gain,
    k0, k1, k2, k3, k4, k5, k6, k7,
    out, edge_out,
    w0, w1, w2, w3, w4, w5, w6, w7,
    send, got, got_ids, acc, part, plane, share, aggregate, base, middle, whole,
    outgoing, halo, pre_all, incoming, newest, update,
    s_msg, r_msg, s_ids, r_ids, s_z, r_z, s_share, r_share, s_base, r_base, s_mid, r_mid,
    s_halo, r_halo, s_inc, r_inc, s_new, r_new,
    s_part, r_part, s_cross, r_cross, s_fwd, r_fwd,
):
    pieces = (k0, k1, k2, k3, k4, k5, k6, k7)
    weights = (w0, w1, w2, w3, w4, w5, w6, w7)
    lat = lax.axis_index("lat")
    lon = lax.axis_index("lon")
    z = lat // 8
    cell = lat % 8
    place = cell * LON + lon
    owner = z % 4 == lon

    def at_place(t):
        return {"lat": z * 8 + t // LON, "lon": t % LON}

    def at_depth(depth):
        return {"lat": depth * 8 + cell, "lon": lon}

    def at_lon(other):
        return {"lat": lat, "lon": other}

    def beside(step):
        return at_lon((lon + step) % LON)

    def behind(step):
        return (lon - step + LON) % LON

    def rows_of(q):
        return pl.ds(pl.multiple_of(q * ROWS, ROWS), ROWS)

    mine = rows_of(lon)
    barrier = pltpu.get_barrier_semaphore()

    def greet(d, _):
        pl.semaphore_signal(
            barrier, inc=1, device_id={"lat": (lat + d) % LAT, "lon": lon}, device_id_type=MESH
        )
        return 0

    lax.fori_loop(1, LAT, greet, 0)
    for step in range(1, LON):

        def greet_plane(c, _):
            pl.semaphore_signal(
                barrier,
                inc=1,
                device_id={"lat": z * 8 + (cell + c) % 8, "lon": (lon + step) % LON},
                device_id_type=MESH,
            )
            return 0

        lax.fori_loop(0, 8, greet_plane, 0)

    def target(d):
        return (place + d) % PLANE

    def pick(s, _):
        one, two = target(2 * s), target(2 * s + 1)
        names = jnp.concatenate([idx[one][0:1, :], idx[two][0:1, :]], axis=1)
        rows = matmul_t(one_hot(names, WIDTH), grid[...]).astype(BF16)
        send[2 * s] = rows[:128]
        send[2 * s + 1] = rows[128:]
        return 0

    def compute(d):
        one, two = target(d), target(d + 1)
        features = jnp.concatenate([feat[one], feat[two]], axis=1).astype(BF16)
        rows = jnp.concatenate([send[d], send[d + 1]], axis=0)
        pre = matmul(rows, w0[...]) + (matmul_t(features, proj[...]) + edge_bias[0:1, :])
        raw = matmul_nt(swish(pre).astype(BF16), w1[...])
        message = layer_norm(raw, edge_gain[...], edge_bias[1:2, :]).astype(BF16)
        send[d] = message[:128]
        send[d + 1] = message[128:]

    def message_copy(d):
        return remote(send.at[d], got.at[d], s_msg.at[d], r_msg.at[d], at_place(target(d)))

    def ids_copy(d):
        return remote(idx.at[target(d)], got_ids.at[d], s_ids.at[d], r_ids.at[d], at_place(target(d)))

    def base_copy(step, writer):
        return remote(
            mesh.at[rows_of((lon + step) % LON), :],
            base.at[:, rows_of(writer)],
            s_base.at[step],
            r_base.at[step],
            beside(step),
        )

    partner = lon + 1 - 2 * (lon % 2)
    cross = (lon + 2) % LON
    corner = partner + 2 - 4 * (partner // 2)

    def block(i, q):
        return weights[i].at[:, rows_of(q)] if COLUMNS[i] else weights[i].at[rows_of(q), :]

    def to_partner(i, q):
        return remote(pieces[i], block(i, q), s_part.at[i], r_part.at[i], at_lon(partner))

    def to_cross(i, q):
        return remote(pieces[i], block(i, q), s_cross.at[i], r_cross.at[i], at_lon(cross))

    def forward(i, q):
        return remote(block(i, q), block(i, q), s_fwd.at[i], r_fwd.at[i], at_lon(partner))

    def offer(i):
        to_cross(i, lon).start()
        to_partner(i, lon).start()

    def relay(i):
        to_cross(i, cross).wait_recv()
        forward(i, cross).start()

    def settle(i):
        to_partner(i, partner).wait_recv()
        forward(i, corner).wait_recv()

    lax.fori_loop(0, 4, pick, 0)
    pl.semaphore_wait(barrier, LAT - 1 + 24)
    offer(0)
    offer(1)

    def start_ids(d, _):
        ids_copy(d).start()
        return 0

    lax.fori_loop(1, PLANE, start_ids, 0)
    for step in range(1, LON):
        base_copy(step, lon).start()
    for i in range(8):
        if COLUMNS[i]:
            weights[i][:, mine] = pieces[i][...]
        else:
            weights[i][mine, :] = pieces[i][...]
    base[:, mine] = mesh[mine, :]
    lax.fori_loop(4, PLANE // 2, pick, 0)
    relay(0)
    relay(1)
    settle(0)
    settle(1)

    compute(0)
    got[0] = send[0]
    got_ids[0] = idx[place]
    message_copy(1).start()

    def start_messages(s, _):
        compute(2 * s)
        message_copy(2 * s).start()
        message_copy(2 * s + 1).start()
        return 0

    lax.fori_loop(1, PLANE // 2, start_messages, 0)
    for i in range(2, 8):
        offer(i)

    acc[...] = jnp.zeros_like(acc)

    def take(g):
        ids = jnp.concatenate([got_ids[4 * g + i][1:2, :] for i in range(4)], axis=1)
        rows = jnp.concatenate([got[4 * g + i] for i in range(4)], axis=0)
        acc[...] += matmul(one_hot(ids, 2 * NODES), rows)

    def arrive(d):
        ids_copy(d).wait_recv()
        message_copy(d).wait_recv()

    for d in range(1, 4):
        arrive(d)
    take(0)

    def collect(g, _):
        for i in range(4):
            arrive(4 * g + i)
        take(g)
        return 0

    lax.fori_loop(1, PLANE // 4, collect, 0)

    def depth_copy(j, q):
        depth = lon + 4 * j
        away = (depth - z + DEPTH) % DEPTH
        return remote(
            part.at[pl.ds(j * NODES + q * ROWS, ROWS), :],
            plane.at[away, pl.ds(q * ROWS, ROWS), :],
            s_z.at[j, q],
            r_z.at[away, q],
            at_depth(depth),
        )

    for q in range(LON):
        for j in range(2):
            rows = pl.ds(j * NODES + q * ROWS, ROWS)
            part[rows, :] = acc[rows, :].astype(BF16)

            @pl.when(z != lon + 4 * j)
            def _():
                depth_copy(j, q).start()

    relay(2)
    relay(3)

    def share_copy(q):
        return remote(share.at[q], aggregate, s_share.at[q], r_share.at[0], at_lon(q))

    @pl.when(owner)
    def _():
        for q in range(LON):
            first = pl.multiple_of((z // 4) * NODES + q * ROWS, ROWS)
            total = acc[pl.ds(first, ROWS), :]
            for away in range(1, DEPTH):
                remote(
                    part.at[pl.ds(0, ROWS), :],
                    plane.at[away, pl.ds(q * ROWS, ROWS), :],
                    s_z.at[0, q],
                    r_z.at[away, q],
                    at_depth(z),
                ).wait_recv()
                total = total + plane[away, pl.ds(q * ROWS, ROWS), :].astype(F32)
            rounded = total.astype(BF16)

            @pl.when(lon == q)
            def _():
                aggregate[...] = rounded

            @pl.when(lon != q)
            def _():
                share[q] = rounded
                share_copy(q).start()

    settle(2)
    settle(3)
    for step in range(1, LON):
        base_copy(step, behind(step)).wait_recv()

    def node_network(before, pre_base, summed, w_in, w_out, bias, gain):
        pre = pre_base + matmul(summed, w_in[WIDTH:, :]) + bias[0:1, :]
        raw = matmul(swish(pre).astype(BF16), w_out[...])
        return (before.astype(F32) + layer_norm(raw, gain[...], bias[1:2, :])).astype(BF16)

    pre_base = matmul(base[...], w2[:WIDTH, :])

    @pl.when(z % 4 != lon)
    def _():
        share_copy(0).wait_recv()

    middle[...] = node_network(base[...], pre_base, aggregate[...], w2, w3, node_bias, node_gain)

    def middle_copy(step, writer):
        return remote(middle, whole.at[rows_of(writer), :], s_mid.at[step], r_mid.at[step], beside(step))

    for step in range(1, LON):
        middle_copy(step, lon).start()
    whole[mine, :] = middle[...]
    for i in range(4, 8):
        relay(i)
    for step in range(1, LON):
        middle_copy(step, behind(step)).wait_recv()

    chosen = matmul_t(one_hot(halo_rows[...], NODES), whole[...])
    outgoing[...] = chosen.reshape(LAT, 8, WIDTH).astype(BF16)

    def halo_copy(d, writer):
        other = (lat + d) % LAT
        return remote(
            outgoing.at[other], halo.at[writer], s_halo.at[d], r_halo.at[d], {"lat": other, "lon": lon}
        )

    def start_halo(d, _):
        halo_copy(d, lat).start()
        return 0

    lax.fori_loop(1, LAT, start_halo, 0)
    halo[lat] = outgoing[lat]
    for i in range(4, 8):
        settle(i)

    def begin(c, _):
        rows = pl.ds(pl.multiple_of(c * 256, 256), 256)
        sent = matmul_t(one_hot(sender[c], NODES), whole[...]).astype(BF16)
        received = matmul_t(one_hot(receiver[c], NODES), whole[...]).astype(BF16)
        pre = matmul(edges[rows, :], w4[:WIDTH, :])
        pre = pre + matmul(sent, w4[WIDTH : 2 * WIDTH, :])
        pre = pre + matmul(received, w4[2 * WIDTH :, :])
        pre_all[rows, :] = pre + proc_bias[0:1, :]
        return 0

    lax.fori_loop(0, 4, begin, 0)
    last_base = matmul(middle[...], w6[:WIDTH, :])

    def end_halo(d, _):
        halo_copy(d, (lat - d + LAT) % LAT).wait_recv()
        return 0

    lax.fori_loop(1, LAT, end_halo, 0)
    incoming[...] = jnp.zeros_like(incoming)
    table = halo[...].astype(F32).reshape(NODES, WIDTH).astype(BF16)

    def finish(c, _):
        rows = pl.ds(pl.multiple_of(c * 256, 256), 256)
        sent = matmul_t(one_hot(sender[c] - NODES, NODES), table).astype(BF16)
        pre = pre_all[rows, :] + matmul(sent, w4[WIDTH : 2 * WIDTH, :])
        raw = matmul_nt(swish(pre).astype(BF16), w5[...])
        old = edges[rows, :].astype(F32)
        updated = (old + layer_norm(raw, proc_gain[...], proc_bias[1:2, :])).astype(BF16)
        edge_out[rows, :] = updated
        incoming[...] += matmul(one_hot(receiver[c], NODES), updated)
        return 0

    lax.fori_loop(0, 4, finish, 0)
    for q in range(LON):
        for j in range(2):

            @pl.when(z != lon + 4 * j)
            def _():
                depth_copy(j, q).wait_send()

    for q in range(LON):
        share_rows = pl.ds(q * ROWS, ROWS)
        part[share_rows, :] = incoming[share_rows, :].astype(BF16)

    def incoming_copy(step):
        return remote(
            part.at[rows_of((lon + step) % LON), :],
            plane.at[0, pl.ds(step * ROWS, ROWS), :],
            s_inc.at[step],
            r_inc.at[step],
            beside(step),
        )

    for step in range(1, LON):
        incoming_copy(step).start()
    total = incoming[mine, :]
    for step in range(1, LON):
        incoming_copy(step).wait_recv()
        total = total + plane[0, step * ROWS : (step + 1) * ROWS, :].astype(F32)
    newest[...] = node_network(middle[...], last_base, total.astype(BF16), w6, w7, last_bias, last_gain)

    def newest_copy(step, writer):
        return remote(
            newest.at[:, rows_of((lon + step) % LON)],
            update.at[rows_of(writer), :],
            s_new.at[step],
            r_new.at[step],
            beside(step),
        )

    for step in range(1, LON):
        newest_copy(step, lon).start()
    update[mine, :] = newest[:, mine]

    def sent(d, _):
        ids_copy(d).wait_send()
        message_copy(d).wait_send()
        return 0

    lax.fori_loop(1, PLANE, sent, 0)

    def sent_halo(d, _):
        halo_copy(d, lat).wait_send()
        return 0

    lax.fori_loop(1, LAT, sent_halo, 0)
    for i in range(8):
        to_cross(i, lon).wait_send()
        to_partner(i, lon).wait_send()
        forward(i, cross).wait_send()
    for step in range(1, LON):
        base_copy(step, lon).wait_send()
        middle_copy(step, lon).wait_send()
        incoming_copy(step).wait_send()
        newest_copy(step, lon).wait_send()

    @pl.when(owner)
    def _():
        for q in range(LON):

            @pl.when(lon != q)
            def _():
                share_copy(q).wait_send()

    for step in range(1, LON):
        newest_copy(step, behind(step)).wait_recv()
    out[...] = update[...]


def layer(*operands):
    dma = pltpu.SemaphoreType.DMA
    shapes = [
        (WIDTH, WIDTH), (WIDTH, WIDTH), (2 * WIDTH, WIDTH), (WIDTH, WIDTH),
        (3 * WIDTH, WIDTH), (WIDTH, WIDTH), (2 * WIDTH, WIDTH), (WIDTH, WIDTH),
        (PLANE, 128, WIDTH), (PLANE, 128, WIDTH),
    ]
    return pl.pallas_call(
        layer_kernel,
        in_specs=[pl.BlockSpec(memory_space=pltpu.VMEM)] * len(operands),
        out_specs=[pl.BlockSpec(memory_space=pltpu.VMEM)] * 2,
        out_shape=[
            jax.ShapeDtypeStruct((NODES, ROWS), BF16),
            jax.ShapeDtypeStruct((1024, WIDTH), BF16),
        ],
        scratch_shapes=[pltpu.VMEM(shape, BF16) for shape in shapes]
        + [
            pltpu.VMEM((PLANE, 2, 128), jnp.int32),
            pltpu.VMEM((2 * NODES, WIDTH), F32),
            pltpu.VMEM((2 * NODES, WIDTH), BF16),
            pltpu.VMEM((DEPTH, NODES, WIDTH), BF16),
            pltpu.VMEM((LON, ROWS, WIDTH), BF16),
            pltpu.VMEM((ROWS, WIDTH), BF16),
            pltpu.VMEM((ROWS, WIDTH), BF16),
            pltpu.VMEM((ROWS, WIDTH), BF16),
            pltpu.VMEM((NODES, WIDTH), BF16),
            pltpu.VMEM((LAT, 8, WIDTH), BF16),
            pltpu.VMEM((LAT, 8, WIDTH), BF16),
            pltpu.VMEM((1024, WIDTH), F32),
            pltpu.VMEM((NODES, WIDTH), F32),
            pltpu.VMEM((ROWS, WIDTH), BF16),
            pltpu.VMEM((NODES, ROWS), BF16),
            dma((PLANE,)), dma((PLANE,)), dma((PLANE,)), dma((PLANE,)),
            dma((2, LON)), dma((DEPTH, LON)), dma((LON,)), dma((1,)),
            dma((LON,)), dma((LON,)), dma((LON,)), dma((LON,)),
            dma((LAT,)), dma((LAT,)), dma((LON,)), dma((LON,)), dma((LON,)), dma((LON,)),
            dma((8,)), dma((8,)), dma((8,)), dma((8,)), dma((8,)), dma((8,)),
        ],
        compiler_params=pltpu.CompilerParams(
            collective_id=0, has_side_effects=True, vmem_limit_bytes=60 * 1024 * 1024
        ),
        name="layer",
    )(*operands)


def local(
    grid_latent,
    grid_feat,
    grid_sender,
    grid_owner,
    grid_node,
    mesh_latent,
    mesh_edge,
    halo_send,
    mesh_sender,
    mesh_receiver,
    enc_edge_in,
    enc_feat_proj,
    enc_edge_out,
    enc_edge_bias,
    enc_edge_gain,
    enc_node_in,
    enc_node_out,
    enc_node_bias,
    enc_node_gain,
    proc_edge_in,
    proc_edge_out,
    proc_edge_bias,
    proc_edge_gain,
    proc_node_in,
    proc_node_out,
    proc_node_bias,
    proc_node_gain,
):
    idx, fields = slots(
        grid_owner.reshape(1, -1), grid_sender.reshape(1, -1), grid_node.reshape(1, -1), grid_feat
    )
    proj = jnp.concatenate([enc_feat_proj, jnp.zeros((4, WIDTH), BF16)], 0)
    return layer(
        idx.reshape(PLANE, 2, 128),
        fields.reshape(PLANE, 8, 128),
        grid_latent,
        mesh_latent,
        halo_send.reshape(1, -1),
        mesh_edge,
        mesh_sender.reshape(4, 1, 256),
        mesh_receiver.reshape(4, 1, 256),
        proj,
        enc_edge_bias,
        enc_edge_gain[None],
        enc_node_bias,
        enc_node_gain[None],
        proc_edge_bias,
        proc_edge_gain[None],
        proc_node_bias,
        proc_node_gain[None],
        enc_edge_in,
        enc_edge_out,
        enc_node_in,
        enc_node_out,
        proc_edge_in,
        proc_edge_out,
        proc_node_in,
        proc_node_out,
    )


def solution(mesh):
    placed = (
        P(("lat", "lon"), None),
        P(None, ("lat", "lon")),
        P(("lat", "lon")),
        P(("lat", "lon"), None),
        P(("lat", "lon")),
        P("lat", "lon"),
        P(("lat", "lon"), None),
        P("lat", None),
        P(("lat", "lon")),
        P(("lat", "lon")),
        P(None, "lon"),
        P(),
        P(None, "lon"),
        P(),
        P(),
        P(None, "lon"),
        P("lon", None),
        P(),
        P(),
        P(None, "lon"),
        P(None, "lon"),
        P(),
        P(),
        P(None, "lon"),
        P("lon", None),
        P(),
        P(),
    )
    return jax.shard_map(
        local,
        mesh=mesh,
        in_specs=placed,
        out_specs=(P("lat", "lon"), P(("lat", "lon"), None)),
        check_vma=False,
    )
```

time: 316 us -> 189 us (0.60)
  waiting for transfers between devices: 110 us -> 0 us
  Pallas kernels: 142 us -> 179 us
  local copies, waits for them, and re-layouts: 24.3 us -> 8.93 us
  between operations: 13.8 us -> 0.65 us
  starting transfers between devices: 11.7 us -> 0 us
  blocking collectives: 7.08 us -> 0 us
  other arithmetic: 5.62 us -> 0 us
    all_gather x3 -> x0, waiting for transfers between devices: 91.3 us -> none  [the longest x1 50.7 us: local(): lax.all_gather(jnp.concatenate([enc_node_in, proc_edge_in, proc_edge_out,...]
    pallas_call x3 -> x1, Pallas kernels: 139 us -> 176 us  [layer(): pl.pallas_call(layer_kernel, in_specs=[pl.BlockSpec(memory_space=pltpu.VM...]
    all_to_all x2 -> x0, waiting for transfers between devices: 19 us -> none  [swap(): return lax.all_to_all(tiles, axis, split_axis=0, concat_axis=0, tiled=True)]
    slice x5 -> x0, local copies, waits for them, and re-layouts: 12.1 us -> none  [the longest x1 2.99 us: local(): inner[3072:]]
    all_to_all x2 -> x0, starting transfers between devices: 11.6 us -> none  [swap(): return lax.all_to_all(tiles, axis, split_axis=0, concat_axis=0, tiled=True)]
    all_to_all x1 -> x0, blocking collectives: 7.08 us -> none  [swap(): return lax.all_to_all(tiles, axis, split_axis=0, concat_axis=0, tiled=True)]
    concatenate x3 -> x0, other arithmetic: 5.61 us -> none  [the longest x1 2.25 us: local(): jnp.concatenate([enc_node_in, proc_edge_in, proc_edge_out, proc_node_in], 0)]
    gather x1 -> x0, local copies, waits for them, and re-layouts: 3.76 us -> none  [local(): halo = swap(mesh_mid[halo_send], 'lat').reshape(NODES, WIDTH)]
  transfers between devices with their start and end apart: 5 -> 0, of which waited for: 5 -> 0; matrix products, arithmetic and copies ran while one was open for 6% -> 0% of each run, Pallas kernels for 1% -> 0%
where the time goes in v3:
time: 189 us; the launch traced here: 188 us
  Pallas kernels  179 us (95%)
  local copies, waits for them, and re-layouts  8.93 us (5%)
    pallas_call x1, Pallas kernels, layer(): pl.pallas_call(layer_kernel, in_specs=[pl.BlockSpec(memory_space=pltpu.VM...  176 us
    unnamed x8, local copies, waits for them, and re-layouts  6.27 us

profile of v3, /device:TPU:1, one launch (start us, length us, event | category | flops | bytes accessed | tf_op | source)
XLA Modules:
  0.0 188.4 jit_solution(15748768087955337454)
XLA Ops:
  0.6 0.0 copy-start
  0.6 0.7 copy-done
  1.3 0.0 copy-start.1
  1.3 0.6 concatenate.3.proj
  1.9 0.1 copy-done.1
  2.0 0.1 copy.30
  2.1 0.7 reshape.33.halo_rows
  2.8 3.2 %slots.1 = (s32[32,256]{1,0:T(8,128)}, f32[32,1024]{1,0:T(8,128)}) custom-call(s32[1,2048]{1,0:T(1,128)} %bitcast.13, s32[1,2048]{1,0:T(1,128)} %bitcast.14, s32[1,2048]{1,0:T(1,128)} %bitcast.15, bf16[4,2048]{1,0:T(4,128)(2,1)} %feat.1), custom_call_target="tpu_custom_call" | custom-call | tf_op jit(solution)/shard_map/slots/pallas_call | solution.py:86
  6.0 1.4 reshape.31.idx
  7.4 1.6 copy.31
  8.9 175.7 %layer.1 = (bf16[512,128]{1,0:T(8,128)(2,1)}, bf16[1024,512]{1,0:T(8,128)(2,1)}) custom-call(s32[32,2,128]{2,1,0:T(2,128)} %reshape.31.idx, f32[32,8,128]{2,1,0:T(8,128)} %bitcast.11, bf16[512,512]{1,0:T(8,128)(2,1)} %grid.1, bf16[512,128]{1,0:T(8,128)(2,1)} %mesh.1, s32[1,512]{1,0:T(1,128)} %reshape.33.halo_rows, bf16[1024,512]{1,0:T(8,128)(2,1)} %edges.1, ...), custom_call_target="tpu_custom_call" | custom-call | tf_op jit(solution)/shard_map/layer/pallas_call | solution.py:512
  184.6 1.6 copy.34
  186.2 2.3 %copy.35 = bf16[1024,512]{1,0:T(8,128)(2,1)} copy(bf16[1024,512]{1,0:T(8,128)(2,1)} %get-tuple-element.9) | data formatting | bytes 2097152
Async XLA Ops:
  0.6 0.7 copy-start
  1.3 0.7 copy-start.1

commit v4 on v3

--- a/solution.py
+++ b/solution.py
@@ -15,6 +15,7 @@
 ROWS = NODES // LON
 PLANE = 32
 DEPTH = 8
+HALF = WIDTH // 2
 MESH = pl.DeviceIdType.MESH
 
 
@@ -64,7 +65,7 @@
         carry = carry + jnp.sum(wide, axis=1, keepdims=True)
     rank = jnp.concatenate(ranks, axis=1).astype(jnp.int32)
     half = owners // 32
-    target = (owners % 8) * 4 + (owners // 8) % 4
+    target = (owners % 8) * 4 + (owners // 8) % 2 * 2 + (owners // 16) % 2
     at_target = one_hot(target, PLANE)
     place = one_hot(rank + half * CAP, 2 * CAP).astype(F32)
     named = node[...] + half * NODES + 1
@@ -126,7 +127,8 @@
     z = lat // 8
     cell = lat % 8
     place = cell * LON + lon
-    owner = z % 4 == lon
+    shelf = 2 * (lon % 2) + lon // 2
+    owner = z % 4 == shelf
 
     def at_place(t):
         return {"lat": z * 8 + t // LON, "lon": t % LON}
@@ -170,7 +172,10 @@
         lax.fori_loop(0, 8, greet_plane, 0)
 
     def target(d):
-        return (place + d) % PLANE
+        turn = (d * 13) % PLANE
+        row = (place // 8 + turn // 8) % 4
+        column = (place // 2 + turn // 2) % 4
+        return row * 8 + column * 2 + (place + turn) % 2
 
     def pick(s, _):
         one, two = target(2 * s), target(2 * s + 1)
@@ -190,8 +195,15 @@
         send[d] = message[:128]
         send[d + 1] = message[128:]
 
-    def message_copy(d):
-        return remote(send.at[d], got.at[d], s_msg.at[d], r_msg.at[d], at_place(target(d)))
+    def message_copy(d, half):
+        columns = pl.ds(half * HALF, HALF)
+        return remote(
+            send.at[d, :, columns],
+            got.at[d, :, columns],
+            s_msg.at[half, d],
+            r_msg.at[half, d],
+            at_place(target(d)),
+        )
 
     def ids_copy(d):
         return remote(idx.at[target(d)], got_ids.at[d], s_ids.at[d], r_ids.at[d], at_place(target(d)))
@@ -260,58 +272,76 @@
     compute(0)
     got[0] = send[0]
     got_ids[0] = idx[place]
-    message_copy(1).start()
+    message_copy(1, 0).start()
 
     def start_messages(s, _):
         compute(2 * s)
-        message_copy(2 * s).start()
-        message_copy(2 * s + 1).start()
+        message_copy(2 * s, 0).start()
+        message_copy(2 * s + 1, 0).start()
         return 0
 
     lax.fori_loop(1, PLANE // 2, start_messages, 0)
+
+    def start_rest(d, _):
+        message_copy(d, 1).start()
+        return 0
+
+    lax.fori_loop(1, PLANE, start_rest, 0)
     for i in range(2, 8):
         offer(i)
 
     acc[...] = jnp.zeros_like(acc)
 
-    def take(g):
+    def take(g, half):
+        columns = slice(half * HALF, (half + 1) * HALF)
         ids = jnp.concatenate([got_ids[4 * g + i][1:2, :] for i in range(4)], axis=1)
-        rows = jnp.concatenate([got[4 * g + i] for i in range(4)], axis=0)
-        acc[...] += matmul(one_hot(ids, 2 * NODES), rows)
-
-    def arrive(d):
-        ids_copy(d).wait_recv()
-        message_copy(d).wait_recv()
-
-    for d in range(1, 4):
-        arrive(d)
-    take(0)
-
-    def collect(g, _):
-        for i in range(4):
-            arrive(4 * g + i)
-        take(g)
-        return 0
-
-    lax.fori_loop(1, PLANE // 4, collect, 0)
+        rows = jnp.concatenate([got[4 * g + i, :, columns] for i in range(4)], axis=0)
+        acc[:, columns] += matmul(one_hot(ids, 2 * NODES), rows)
+
+    def arrive(d, half):
+        if half == 0:
+            ids_copy(d).wait_recv()
+        message_copy(d, half).wait_recv()
+
+    def collect(half):
+        for d in range(1, 4):
+            arrive(d, half)
+        take(0, half)
+
+        def group(g, _):
+            for i in range(4):
+                arrive(4 * g + i, half)
+            take(g, half)
+            return 0
+
+        lax.fori_loop(1, PLANE // 4, group, 0)
 
     def depth_copy(j, q):
-        depth = lon + 4 * j
+        depth = shelf + 4 * j
         away = (depth - z + DEPTH) % DEPTH
-        return remote(
-            part.at[pl.ds(j * NODES + q * ROWS, ROWS), :],
-            plane.at[away, pl.ds(q * ROWS, ROWS), :],
-            s_z.at[j, q],
-            r_z.at[away, q],
-            at_depth(depth),
-        )
-
+        if q == LON:
+            source = part.at[pl.ds(j * NODES, NODES), pl.ds(0, HALF)]
+            goal = plane.at[away, :, pl.ds(0, HALF)]
+        else:
+            source = part.at[pl.ds(j * NODES + q * ROWS, ROWS), pl.ds(HALF, HALF)]
+            goal = plane.at[away, pl.ds(q * ROWS, ROWS), pl.ds(HALF, HALF)]
+        return remote(source, goal, s_z.at[j, q], r_z.at[away, q], at_depth(depth))
+
+    collect(0)
+    part[:, :HALF] = acc[:, :HALF].astype(BF16)
+    for j in range(2):
+
+        @pl.when(z != shelf + 4 * j)
+        def _():
+            depth_copy(j, LON).start()
+
+    collect(1)
     for q in range(LON):
         for j in range(2):
             rows = pl.ds(j * NODES + q * ROWS, ROWS)
-            part[rows, :] = acc[rows, :].astype(BF16)
-
-            @pl.when(z != lon + 4 * j)
+            part[rows, HALF:] = acc[rows, HALF:].astype(BF16)
+
+            @pl.when(z != shelf + 4 * j)
             def _():
                 depth_copy(j, q).start()
 
@@ -321,19 +351,24 @@
     def share_copy(q):
         return remote(share.at[q], aggregate, s_share.at[q], r_share.at[0], at_lon(q))
 
+    def depth_arrival(away, q):
+        if q == LON:
+            source = part.at[pl.ds(0, NODES), pl.ds(0, HALF)]
+            goal = plane.at[away, :, pl.ds(0, HALF)]
+        else:
+            source = part.at[pl.ds(0, ROWS), pl.ds(HALF, HALF)]
+            goal = plane.at[away, pl.ds(q * ROWS, ROWS), pl.ds(HALF, HALF)]
+        return remote(source, goal, s_z.at[0, q], r_z.at[away, q], at_depth(z))
+
     @pl.when(owner)
     def _():
+        for away in range(1, DEPTH):
+            depth_arrival(away, LON).wait_recv()
         for q in range(LON):
             first = pl.multiple_of((z // 4) * NODES + q * ROWS, ROWS)
             total = acc[pl.ds(first, ROWS), :]
             for away in range(1, DEPTH):
-                remote(
-                    part.at[pl.ds(0, ROWS), :],
-                    plane.at[away, pl.ds(q * ROWS, ROWS), :],
-                    s_z.at[0, q],
-                    r_z.at[away, q],
-                    at_depth(z),
-                ).wait_recv()
+                depth_arrival(away, q).wait_recv()
                 total = total + plane[away, pl.ds(q * ROWS, ROWS), :].astype(F32)
             rounded = total.astype(BF16)
 
@@ -358,7 +393,7 @@
 
     pre_base = matmul(base[...], w2[:WIDTH, :])
 
-    @pl.when(z % 4 != lon)
+    @pl.when(z % 4 != shelf)
     def _():
         share_copy(0).wait_recv()
 
@@ -426,10 +461,10 @@
         return 0
 
     lax.fori_loop(0, 4, finish, 0)
-    for q in range(LON):
+    for q in range(LON + 1):
         for j in range(2):
 
-            @pl.when(z != lon + 4 * j)
+            @pl.when(z != shelf + 4 * j)
             def _():
                 depth_copy(j, q).wait_send()
 
@@ -469,7 +504,8 @@
 
     def sent(d, _):
         ids_copy(d).wait_send()
-        message_copy(d).wait_send()
+        message_copy(d, 0).wait_send()
+        message_copy(d, 1).wait_send()
         return 0
 
     lax.fori_loop(1, PLANE, sent, 0)
@@ -534,8 +570,8 @@
             pltpu.VMEM((NODES, WIDTH), F32),
             pltpu.VMEM((ROWS, WIDTH), BF16),
             pltpu.VMEM((NODES, ROWS), BF16),
-            dma((PLANE,)), dma((PLANE,)), dma((PLANE,)), dma((PLANE,)),
-            dma((2, LON)), dma((DEPTH, LON)), dma((LON,)), dma((1,)),
+            dma((2, PLANE)), dma((2, PLANE)), dma((PLANE,)), dma((PLANE,)),
+            dma((2, LON + 1)), dma((DEPTH, LON + 1)), dma((LON,)), dma((1,)),
             dma((LON,)), dma((LON,)), dma((LON,)), dma((LON,)),
             dma((LAT,)), dma((LAT,)), dma((LON,)), dma((LON,)), dma((LON,)), dma((LON,)),
             dma((8,)), dma((8,)), dma((8,)), dma((8,)), dma((8,)), dma((8,)),

time: 189 us -> 163 us (0.86)
  Pallas kernels: 179 us -> 153 us
    pallas_call x1, Pallas kernels: 176 us -> 150 us  [layer(): pl.pallas_call(layer_kernel, in_specs=[pl.BlockSpec(memory_space=pltpu.VM...]
where the time goes in v4:
time: 163 us; the launch traced here: 162 us
  Pallas kernels  153 us (94%)
  local copies, waits for them, and re-layouts  8.93 us (5%)
    pallas_call x1, Pallas kernels, layer(): pl.pallas_call(layer_kernel, in_specs=[pl.BlockSpec(memory_space=pltpu.VM...  150 us
    unnamed x8, local copies, waits for them, and re-layouts  6.27 us

profile of v4, /device:TPU:1, one launch (start us, length us, event | category | flops | bytes accessed | tf_op | source)
XLA Modules:
  0.0 162.5 jit_solution(11128768387208526817)
XLA Ops:
  0.6 0.0 copy-start
  0.6 0.7 copy-done
  1.3 0.0 copy-start.1
  1.3 0.6 concatenate.3.proj
  1.9 0.1 copy-done.1
  2.0 0.1 copy.30
  2.1 0.7 reshape.33.halo_rows
  2.8 3.2 %slots.1 = (s32[32,256]{1,0:T(8,128)}, f32[32,1024]{1,0:T(8,128)}) custom-call(s32[1,2048]{1,0:T(1,128)} %bitcast.13, s32[1,2048]{1,0:T(1,128)} %bitcast.14, s32[1,2048]{1,0:T(1,128)} %bitcast.15, bf16[4,2048]{1,0:T(4,128)(2,1)} %feat.1), custom_call_target="tpu_custom_call" | custom-call | tf_op jit(solution)/shard_map/slots/pallas_call | solution.py:87
  6.0 1.4 reshape.31.idx
  7.4 1.6 copy.31
  8.9 149.7 %layer.1 = (bf16[512,128]{1,0:T(8,128)(2,1)}, bf16[1024,512]{1,0:T(8,128)(2,1)}) custom-call(s32[32,2,128]{2,1,0:T(2,128)} %reshape.31.idx, f32[32,8,128]{2,1,0:T(8,128)} %bitcast.11, bf16[512,512]{1,0:T(8,128)(2,1)} %grid.1, bf16[512,128]{1,0:T(8,128)(2,1)} %mesh.1, s32[1,512]{1,0:T(1,128)} %reshape.33.halo_rows, bf16[1024,512]{1,0:T(8,128)(2,1)} %edges.1, ...), custom_call_target="tpu_custom_call" | custom-call | tf_op jit(solution)/shard_map/layer/pallas_call | solution.py:548
  158.7 1.6 copy.34
  160.2 2.3 %copy.35 = bf16[1024,512]{1,0:T(8,128)(2,1)} copy(bf16[1024,512]{1,0:T(8,128)(2,1)} %get-tuple-element.9) | data formatting | bytes 2097152
Async XLA Ops:
  0.6 0.7 copy-start
  1.3 0.7 copy-start.1

commit v5 on v4

--- a/solution.py
+++ b/solution.py
@@ -47,7 +47,7 @@
     return (lax.broadcasted_iota(jnp.int32, (count, width), 0) == row).astype(BF16)
 
 
-def slots_kernel(owner, sender, node, feat, idx, fields):
+def fill_slots(owner, sender, node, feat, idx, fields):
     count = owner.shape[1]
     block = 128
     owners = owner[...]
@@ -76,22 +76,15 @@
     def put_whole(values):
         return (put(values // 32) * 32.0 + put(values % 32)).astype(jnp.int32)
 
-    idx[:, :128] = put_whole(sender[...])
-    idx[:, 128:] = put_whole(named) - 1
+    rows = [put_whole(sender[...]), put_whole(named) - 1]
+    for t in range(PLANE):
+        for i in range(2):
+            idx[t, i : i + 1, :] = rows[i][t : t + 1, :]
+    fields[...] = jnp.zeros_like(fields)
     for i in range(4):
-        fields[:, i * 128 : (i + 1) * 128] = put(feat[i : i + 1, :])
-    fields[:, 512:] = jnp.zeros((PLANE, 512), F32)
-
-
-def slots(owner, sender, node, feat):
-    return pl.pallas_call(
-        slots_kernel,
-        out_shape=[
-            jax.ShapeDtypeStruct((PLANE, 256), jnp.int32),
-            jax.ShapeDtypeStruct((PLANE, 1024), F32),
-        ],
-        name="slots",
-    )(owner, sender, node, feat)
+        features = put(feat[i : i + 1, :])
+        for t in range(PLANE):
+            fields[t, i : i + 1, :] = features[t : t + 1, :]
 
 
 def remote(source, target, send, receive, where):
@@ -105,16 +98,17 @@
     )
 
 
+AROUND = (False, True, False, True, False, True, True, True)
 COLUMNS = (True, True, True, False, True, True, True, False)
 
 
 def layer_kernel(
-    idx, feat, grid, mesh, halo_rows, edges, sender, receiver, proj,
+    g_owner, g_sender, g_node, g_feat, grid, mesh, halo_rows, edges, sender, receiver, proj,
     edge_bias, edge_gain, node_bias, node_gain, proc_bias, proc_gain, last_bias, last_gain,
     k0, k1, k2, k3, k4, k5, k6, k7,
     out, edge_out,
     w0, w1, w2, w3, w4, w5, w6, w7,
-    send, got, got_ids, acc, part, plane, share, aggregate, base, middle, whole,
+    send, got, got_ids, idx, feat, acc, part, plane, share, aggregate, base, middle, whole,
     outgoing, halo, pre_all, incoming, newest, update,
     s_msg, r_msg, s_ids, r_ids, s_z, r_z, s_share, r_share, s_base, r_base, s_mid, r_mid,
     s_halo, r_halo, s_inc, r_inc, s_new, r_new,
@@ -228,7 +222,8 @@
         return remote(pieces[i], block(i, q), s_part.at[i], r_part.at[i], at_lon(partner))
 
     def to_cross(i, q):
-        return remote(pieces[i], block(i, q), s_cross.at[i], r_cross.at[i], at_lon(cross))
+        where = {"lat": lat + 1 - 2 * (lat % 2), "lon": cross} if AROUND[i] else at_lon(cross)
+        return remote(pieces[i], block(i, q), s_cross.at[i], r_cross.at[i], where)
 
     def forward(i, q):
         return remote(block(i, q), block(i, q), s_fwd.at[i], r_fwd.at[i], at_lon(partner))
@@ -245,6 +240,7 @@
         to_partner(i, partner).wait_recv()
         forward(i, corner).wait_recv()
 
+    fill_slots(g_owner, g_sender, g_node, g_feat, idx, feat)
     lax.fori_loop(0, 4, pick, 0)
     pl.semaphore_wait(barrier, LAT - 1 + 24)
     offer(0)
@@ -282,13 +278,14 @@
 
     lax.fori_loop(1, PLANE // 2, start_messages, 0)
 
+    offer(2)
+    offer(3)
+
     def start_rest(d, _):
         message_copy(d, 1).start()
         return 0
 
     lax.fori_loop(1, PLANE, start_rest, 0)
-    for i in range(2, 8):
-        offer(i)
 
     acc[...] = jnp.zeros_like(acc)
 
@@ -345,6 +342,8 @@
             def _():
                 depth_copy(j, q).start()
 
+    for i in range(4, 8):
+        offer(i)
     relay(2)
     relay(3)
 
@@ -556,6 +555,8 @@
         scratch_shapes=[pltpu.VMEM(shape, BF16) for shape in shapes]
         + [
             pltpu.VMEM((PLANE, 2, 128), jnp.int32),
+            pltpu.VMEM((PLANE, 2, 128), jnp.int32),
+            pltpu.VMEM((PLANE, 8, 128), F32),
             pltpu.VMEM((2 * NODES, WIDTH), F32),
             pltpu.VMEM((2 * NODES, WIDTH), BF16),
             pltpu.VMEM((DEPTH, NODES, WIDTH), BF16),
@@ -612,13 +613,12 @@
     proc_node_bias,
     proc_node_gain,
 ):
-    idx, fields = slots(
-        grid_owner.reshape(1, -1), grid_sender.reshape(1, -1), grid_node.reshape(1, -1), grid_feat
-    )
     proj = jnp.concatenate([enc_feat_proj, jnp.zeros((4, WIDTH), BF16)], 0)
     return layer(
-        idx.reshape(PLANE, 2, 128),
-        fields.reshape(PLANE, 8, 128),
+        grid_owner.reshape(1, -1),
+        grid_sender.reshape(1, -1),
+        grid_node.reshape(1, -1),
+        grid_feat,
         grid_latent,
         mesh_latent,
         halo_send.reshape(1, -1),

time: 163 us -> 150 us (0.920)
  Pallas kernels: 153 us -> 143 us
  local copies, waits for them, and re-layouts: 8.93 us -> 5.96 us
    pallas_call x1, Pallas kernels: 150 us -> 143 us  [layer(): pl.pallas_call(layer_kernel, in_specs=[pl.BlockSpec(memory_space=pltpu.VM...]
    pallas_call x1 -> x0, Pallas kernels: 3.2 us -> none  [slots(): pl.pallas_call(slots_kernel, out_shape=[jax.ShapeDtypeStruct((PLANE, 256)...]
    unnamed x8 -> x7, local copies, waits for them, and re-layouts: 6.27 us -> 4.68 us
where the time goes in v5:
time: 150 us
  Pallas kernels  143 us (95%)
  local copies, waits for them, and re-layouts  5.96 us (4%)
    pallas_call x1, Pallas kernels, layer(): pl.pallas_call(layer_kernel, in_specs=[pl.BlockSpec(memory_space=pltpu.VM...  143 us
    unnamed x7, local copies, waits for them, and re-layouts  4.68 us

profile of v5, /device:TPU:1, one launch (start us, length us, event | category | flops | bytes accessed | tf_op | source)
XLA Modules:
  0.0 149.7 jit_solution(8841727591124700206)
XLA Ops:
  0.6 0.0 copy-start
  0.6 0.7 copy-done
  1.3 0.0 copy-start.1
  1.3 0.6 concatenate.3.proj
  1.9 0.1 copy-done.1
  2.0 0.1 copy.30
  2.1 0.7 reshape.25.halo_rows
  2.8 143.1 %layer.1 = (bf16[512,128]{1,0:T(8,128)(2,1)}, bf16[1024,512]{1,0:T(8,128)(2,1)}) custom-call(s32[1,2048]{1,0:T(1,128)} %bitcast.9, s32[1,2048]{1,0:T(1,128)} %bitcast.10, s32[1,2048]{1,0:T(1,128)} %bitcast.11, bf16[4,2048]{1,0:T(4,128)(2,1)} %g_feat.1, bf16[512,512]{1,0:T(8,128)(2,1)} %grid.1, bf16[512,128]{1,0:T(8,128)(2,1)} %mesh.1, ...), custom_call_target="tpu_custom_call" | custom-call | tf_op jit(solution)/shard_map/layer/pallas_call | solution.py:547
  145.8 1.6 %copy.33 = bf16[512,128]{1,0:T(8,128)(2,1)} copy(bf16[512,128]{1,0:T(8,128)(2,1)} %get-tuple-element.4) | data formatting | bytes 262144
  147.4 2.3 %copy.34 = bf16[1024,512]{1,0:T(8,128)(2,1)} copy(bf16[1024,512]{1,0:T(8,128)(2,1)} %get-tuple-element.5) | data formatting | bytes 2097152
Async XLA Ops:
  0.6 0.7 copy-start
  1.3 0.7 copy-start.1
